TPU v7x, 128 devices: a whole 4x4x4 slice. The times are simulated.
128 devices in a mesh: face: 8 (over y_lo, x), tile: 16 (over y_hi, z, core).
Axes of the slice: x: 4, y: 4 (y_hi: 2, y_lo: 2; y = y_hi * 2 + y_lo), z: 4, core: 2. Of those that a mesh axis runs over, the one named last changes fastest.
Arguments:
- atmos_state: bfloat16 [128, 1024, 2048], P(None, 'face', 'tile'), may hold values from -6 to 6
- ocean_state: bfloat16 [64, 1024, 2048], P(None, 'face', 'tile'), may hold values from -6 to 6
- land_mask: int32 [1024, 64], P('face', 'tile'), may hold values 0 or 1
- face_turns: int32 [8, 16], P('face', 'tile'), may hold values from 0 to 3
- block_target: int32 [16384, 1], P(('face', 'tile')), may hold values from 0 to 127; in each aligned block of 128 rows (0 to 127, 128 to 255, ...) at most 2 rows name the same one
- block_patch: int32 [16384, 1], P(('face', 'tile')), may hold values from 0 to 127
- block_weight: float32 [16384, 1], P(('face', 'tile')), may hold values from 0.25 to 1
- atmos_w1: bfloat16 [9, 128, 144], replicated, may hold values from -0.15625 to 0.15625
- atmos_w2: bfloat16 [9, 128, 128], replicated, may hold values from -0.1875 to 0.1875
- ocean_w1: bfloat16 [9, 64, 80], replicated, may hold values from -0.21875 to 0.21875
- ocean_w2: bfloat16 [9, 64, 64], replicated, may hold values from -0.25 to 0.25
Outputs:
- atmos_out: bfloat16 [128, 1024, 2048], P(None, 'face', 'tile')
- ocean_out: bfloat16 [64, 1024, 2048], P(None, 'face', 'tile')
Inputs may be any that keep to these rules, and one draw needn't show every extreme that they name: `block_target`: among the 128 blocks of one device, at most 2 have the same target, and in every draw some device has exactly 2 blocks with one target.
All inputs are finite; a program needn't handle non-finite values. No bound on the sum of `land_mask` on one device may be relied on, other than what follows from the above.
Results may differ from a plain program's by a relative error of at most 0.001.
The roundings to bfloat16 on the way count: a program that leaves them out, or rounds other values in their place, can miss the bound.
Values may be sent and summed in bfloat16 or wider, within the bound.
A program may use at most 192 MiB of HBM per device.

v0:
```python
from functools import partial

import jax
import jax.numpy as jnp
from jax import lax
from jax.experimental import pallas as pl
from jax.experimental.pallas import tpu as pltpu
from jax.sharding import PartitionSpec as P

BF = jnp.bfloat16
F32 = jnp.float32
S = 128
CS = 16
MESH = pl.DeviceIdType.MESH
VMEM = pltpu.VMEM
SMEM = pltpu.SMEM

UP, DOWN, LEFT, RIGHT, UL, UR, DL, DR = range(8)
TO_STORED = (
    ((UP, 0), (RIGHT, 0), (DOWN, 1), (LEFT, 1)),
    ((DOWN, 0), (LEFT, 0), (UP, 1), (RIGHT, 1)),
    ((LEFT, 0), (UP, 1), (RIGHT, 1), (DOWN, 0)),
    ((RIGHT, 0), (DOWN, 1), (LEFT, 1), (UP, 0)),
    ((UL, 0), (UR, 1), (DR, 1), (DL, 0)),
    ((UR, 0), (DR, 0), (DL, 1), (UL, 1)),
    ((DL, 0), (UL, 0), (UR, 1), (DR, 1)),
    ((DR, 0), (DL, 1), (UL, 1), (UR, 0)),
)
TO_COMMON = (
    ((UP, 0), (LEFT, 1), (DOWN, 1), (RIGHT, 0)),
    ((DOWN, 0), (RIGHT, 1), (UP, 1), (LEFT, 0)),
    ((LEFT, 0), (DOWN, 0), (RIGHT, 1), (UP, 1)),
    ((RIGHT, 0), (UP, 0), (LEFT, 1), (DOWN, 1)),
)


def anti():
    rows = lax.broadcasted_iota(jnp.int32, (S, S), 0)
    cols = lax.broadcasted_iota(jnp.int32, (S, S), 1)
    return jnp.where(rows + cols == S - 1, 1.0, 0.0).astype(BF)


def eye():
    rows = lax.broadcasted_iota(jnp.int32, (S, S), 0)
    cols = lax.broadcasted_iota(jnp.int32, (S, S), 1)
    return jnp.where(rows == cols, 1.0, 0.0).astype(BF)


def dot(a, b):
    return jnp.dot(a, b, preferred_element_type=F32)


def dot_nt(a, b):
    return lax.dot_general(a, b, (((1,), (1,)), ((), ())), preferred_element_type=F32)


def roll(v, shift):
    return pltpu.roll(v, shift % S, 1)


def lanes(channels):
    return lax.broadcasted_iota(jnp.int32, (channels, S), 1)


def reversed_lanes(v):
    return dot(v, anti()).astype(BF)


def select_sides(table, mode, source, target):
    for turn in range(4):

        @pl.when(mode == turn)
        def _():
            for i, row in enumerate(table):
                side, flip = row[turn]
                v = source[side]
                target[i] = reversed_lanes(v) if flip else v


def ocean_sides(mode, source, target):
    for i in range(8):
        target[i] = source[i]

    @pl.when(mode == 1)
    def _():
        for i in (UP, UL, UR):
            target[i] = jnp.zeros_like(target[i])

    @pl.when(mode == 2)
    def _():
        for i in (DOWN, DL, DR):
            target[i] = reversed_lanes(source[i])


def turn_matrix(v, turns):
    if turns == 1:
        return dot_nt(anti(), v)
    if turns == 2:
        return dot(dot(anti(), v).astype(BF), anti())
    if turns == 3:
        return dot_nt(eye(), dot(anti(), v).astype(BF))
    return v.astype(F32)


def conv_rows(parts, sides, runs, w_ref, outs, carry, finish, flush, unroll):
    first = [lanes(p.shape[1]) == 0 for p in parts]
    last = [lanes(p.shape[1]) == S - 1 for p in parts]
    for side, run in zip(sides, runs):
        run[0] = side[LEFT]
        run[1] = roll(side[LEFT], 64)
        run[2] = roll(side[RIGHT], 1)
        run[3] = roll(side[RIGHT], 65)

    def products(r, first_row, end):
        left, centre, right = [], [], []
        for n, (p, side, run) in enumerate(zip(parts, sides, runs)):
            la, lb, ra, rb = run[0], run[1], run[2], run[3]
            run[0], run[1], run[2], run[3] = roll(la, -1), roll(lb, -1), roll(ra, -1), roll(rb, -1)
            if first_row:
                xa, la, ra = side[UP], side[UL], side[UR]
            else:
                xa = p[r - 1]
            if end is None:
                xb = p[r + 63]
            else:
                xb = jnp.where(end, side[DOWN], p[jnp.minimum(r + 63, S - 1)])
                lb, rb = jnp.where(end, side[DL], lb), jnp.where(end, side[DR], rb)
            both = lambda a, b: jnp.concatenate([a, b], axis=1)
            left.append(both(roll(jnp.where(last[n], la, xa), 1), roll(jnp.where(last[n], lb, xb), 1)))
            centre.append(both(xa, xb))
            right.append(both(roll(jnp.where(first[n], ra, xa), -1), roll(jnp.where(first[n], rb, xb), -1)))
        return dot(w_ref[...], jnp.concatenate(left + centre + right, axis=0))

    o = outs
    p0 = products(0, True, None)
    p1 = products(1, False, None)
    carry[0] = p0[:o] + p1[o : 2 * o]
    carry[1] = p1[:o]

    def sixteen(g, _):
        def body(i, _):
            done, near = carry[0], carry[1]
            for u in range(unroll):
                y = g * 16 + i * unroll + u
                p = products(y + 2, False, y == 63 if u == unroll - 1 else None)
                finish(y, done + p[2 * o :])
                done, near = near + p[o : 2 * o], p[:o]
            carry[0], carry[1] = done, near
            return 0

        lax.fori_loop(0, 16 // unroll, body, 0)
        if flush is not None:
            flush(g)
        return 0

    lax.fori_loop(0, 4, sixteen, 0)


def hidden_kernel(ocean, unroll, count, mode_ref, *refs):
    parts, refs = refs[:count], refs[count:]
    halos, refs = refs[:count], refs[count:]
    w_ref, hid_ref, edge_ref, refs = refs[0], refs[1], refs[2], refs[3:]
    sides, refs = refs[:count], refs[count:]
    runs, refs = refs[:count], refs[count:]
    carry, cols, own = refs
    mode = mode_ref[0]
    for halo, side in zip(halos, sides):
        if ocean:
            ocean_sides(mode, halo, side)
        else:
            select_sides(TO_STORED, mode, halo, side)
    outs = hid_ref.shape[1]
    first, last = lanes(outs) == 0, lanes(outs) == S - 1

    def finish(y, both):
        for half in range(2):
            v = jax.nn.gelu(both[:, half * S : (half + 1) * S], approximate=True).astype(BF)
            hid_ref[y + 64 * half] = v
            cols[half] = roll(jnp.where(first, v, cols[half]), -1)
            cols[2 + half] = jnp.where(last, v, roll(cols[2 + half], -1))

    conv_rows(parts, sides, runs, w_ref, outs, carry, finish, None, unroll)
    upper = lanes(outs) >= 64
    own[UP], own[DOWN] = hid_ref[0], hid_ref[S - 1]
    own[LEFT] = jnp.where(upper, cols[1], roll(cols[0], 64))
    own[RIGHT] = jnp.where(upper, cols[3], roll(cols[2], 64))
    if ocean:
        for i in range(4):
            edge_ref[i] = own[i]
    else:
        select_sides(TO_COMMON, mode, own, edge_ref)


def hidden_conv(ocean, mode, parts, halos, weight, unroll):
    outs = weight.shape[0] // 3
    count = len(parts)
    channels = [p.shape[1] for p in parts]
    vm = pl.BlockSpec(memory_space=VMEM)
    return pl.pallas_call(
        partial(hidden_kernel, ocean, unroll, count),
        out_shape=(
            jax.ShapeDtypeStruct((S, outs, S), BF),
            jax.ShapeDtypeStruct((4, outs, S), BF),
        ),
        in_specs=[pl.BlockSpec(memory_space=SMEM)] + [vm] * (2 * count + 1),
        out_specs=(vm, vm),
        scratch_shapes=[VMEM((8, c, S), BF) for c in channels]
        + [VMEM((4, c, S), BF) for c in channels]
        + [VMEM((2, outs, 2 * S), F32), VMEM((4, outs, S), BF), VMEM((4, outs, S), BF)],
        name="hidden_ocean" if ocean else "hidden_atmos",
    )(mode, *parts, *halos, weight)


def out_kernel(ocean, unroll, mode_ref, hid_ref, halo_ref, w_ref, base_ref, mask_ref, out_ref, side, run, carry, stage):
    mode = mode_ref[0]
    if ocean:
        ocean_sides(mode, halo_ref, side)
    else:
        select_sides(TO_STORED, mode, halo_ref, side)
    outs = hid_ref.shape[1]

    def finish(y, both):
        place = lax.rem(y, 16)
        for half in range(2):
            stage[half, pl.ds(place, outs, stride=16), :] = both[:, half * S : (half + 1) * S]

    def flush(g):
        for half in range(2):
            rows = pl.ds(pl.multiple_of(g * 16 + 64 * half, 16), 16)
            base = base_ref[:, rows, :].astype(F32)
            summed = stage[half].reshape(outs, 16, S)
            if ocean:
                gate = mask_ref[rows, :].astype(F32)[None]
                out_ref[:, rows, :] = (gate * (gate * base + summed)).astype(BF)
            else:
                out_ref[:, rows, :] = (base + summed).astype(BF)

    conv_rows([hid_ref], [side], [run], w_ref, outs, carry, finish, flush, unroll)


def out_conv(ocean, mode, hidden, halo, weight, base, mask, unroll):
    outs = hidden.shape[1]
    vm = pl.BlockSpec(memory_space=VMEM)
    return pl.pallas_call(
        partial(out_kernel, ocean, unroll),
        out_shape=jax.ShapeDtypeStruct((outs, S, S), BF),
        in_specs=[pl.BlockSpec(memory_space=SMEM)] + [vm] * 5,
        out_specs=vm,
        scratch_shapes=[
            VMEM((8, outs, S), BF),
            VMEM((4, outs, S), BF),
            VMEM((2, outs, 2 * S), F32),
            VMEM((2, outs * 16, S), F32),
        ],
        name="out_ocean" if ocean else "out_atmos",
    )(mode, hidden, halo, weight, base, mask)


def prep_kernel(
    turn_ref, target_ref, patch_ref, weight_ref, atmos_ref, surface_ref, ocean_ref, mask_ref,
    xa_ref, xo_ref, ea_ref, eo_ref, pay_ref, meta_ref, common_ref, slot_ref,
    wide_a, wide_o, wide_s, cols_a, cols_o, own, surf, tally, patch_of, weight_of,
):
    step = pl.program_id(0)
    turn = turn_ref[0]

    def columns(cols, v):
        first, last = lanes(v.shape[0]) == 0, lanes(v.shape[0]) == S - 1
        cols[0] = roll(jnp.where(first, v, cols[0]), -1)
        cols[1] = jnp.where(last, v, roll(cols[1], -1))

    @pl.when(step == 0)
    def _():
        pay_ref[...] = jnp.zeros_like(pay_ref)

        def clear(p, _):
            tally[p] = 0
            for n in range(2):
                patch_of[2 * p + n] = 0
                weight_of[2 * p + n] = 0.0
            return 0

        lax.fori_loop(0, S, clear, 0)

    wide_a[...] = atmos_ref[...].astype(F32).reshape(wide_a.shape)
    gate = mask_ref[...].astype(F32)[None]
    wide_o[...] = (ocean_ref[...].astype(F32) * gate).reshape(wide_o.shape)
    for y in range(16):
        v = wide_a[pl.ds(y, S, stride=16), :].astype(BF)
        xa_ref[y] = v
        columns(cols_a, v)
        v = wide_o[pl.ds(y, eo_ref.shape[1], stride=16), :].astype(BF)
        xo_ref[y] = v
        columns(cols_o, v)
        surf[step * 16 + y] = v[:CS]

    @pl.when(step == 0)
    def _():
        own[UP] = xa_ref[0]
        eo_ref[UP] = xo_ref[0]

    @pl.when(step == 7)
    def _():
        own[DOWN], own[LEFT], own[RIGHT] = xa_ref[15], cols_a[0], cols_a[1]
        eo_ref[DOWN], eo_ref[LEFT], eo_ref[RIGHT] = xo_ref[15], cols_o[0], cols_o[1]
        select_sides(TO_COMMON, turn, own, ea_ref)

        def place(b, _):
            goal = target_ref[b]
            seen = tally[goal]
            slot = 2 * goal + seen
            tally[goal] = seen + 1
            slot_ref[b] = slot
            pay_ref[slot] = surf[b]
            patch_of[slot] = patch_ref[b]
            weight_of[slot] = weight_ref[b]
            return 0

        lax.fori_loop(0, S, place, 0)
        lane = lanes(1)

        def describe(p, _):
            places = jnp.where(lane == 0, patch_of[2 * p], patch_of[2 * p + 1]).astype(F32)
            shares = jnp.where(lane == 2, weight_of[2 * p], weight_of[2 * p + 1])
            meta_ref[p] = jnp.where(lane < 2, places, shares)
            return 0

        lax.fori_loop(0, S, describe, 0)
        for quarter in range(4):

            @pl.when(turn == quarter)
            def _():
                for c in range(CS):
                    wide_s[pl.ds(c, S, stride=CS), :] = turn_matrix(surface_ref[c], (4 - quarter) % 4)

        common_ref[...] = wide_s[...].reshape(S, CS, S).astype(BF)


def prepare(turn, target, patch, weight, atmos, ocean, mask):
    ca, co = atmos.shape[0], ocean.shape[0]
    sm = pl.BlockSpec(memory_space=SMEM)
    whole = lambda shape: pl.BlockSpec(shape, lambda i: (0,) * len(shape))
    shape = jax.ShapeDtypeStruct
    return pl.pallas_call(
        prep_kernel,
        grid=(8,),
        out_shape=(
            shape((S, ca, S), BF),
            shape((S, co, S), BF),
            shape((4, ca, S), BF),
            shape((4, co, S), BF),
            shape((2 * S, CS, S), BF),
            shape((S, 1, S), F32),
            shape((S, CS, S), BF),
            shape((S,), jnp.int32),
        ),
        in_specs=[sm] * 4
        + [
            pl.BlockSpec((ca, 16, S), lambda i: (0, i, 0)),
            whole((CS, S, S)),
            pl.BlockSpec((co, 16, S), lambda i: (0, i, 0)),
            pl.BlockSpec((16, S), lambda i: (i, 0)),
        ],
        out_specs=(
            pl.BlockSpec((16, ca, S), lambda i: (i, 0, 0)),
            pl.BlockSpec((16, co, S), lambda i: (i, 0, 0)),
            whole((4, ca, S)),
            whole((4, co, S)),
            whole((2 * S, CS, S)),
            whole((S, 1, S)),
            whole((S, CS, S)),
            sm,
        ),
        scratch_shapes=[
            VMEM((ca * 16, S), F32),
            VMEM((co * 16, S), F32),
            VMEM((S * CS, S), F32),
            VMEM((2, ca, S), BF),
            VMEM((2, co, S), BF),
            VMEM((4, ca, S), BF),
            VMEM((S, CS, S), BF),
            SMEM((S,), jnp.int32),
            SMEM((2 * S,), jnp.int32),
            SMEM((2 * S,), F32),
        ],
        name="prepare",
    )(turn, target, patch, weight, atmos, atmos, ocean, mask)


def remap_kernel(
    turn_ref, patch_ref, weight_ref, in_ref, common_ref, sea_ref, es_ref, back_ref, total, share, cols
):
    turn = turn_ref[0]
    total[...] = jnp.zeros_like(total)

    def clear(p, _):
        share[p] = 0.0
        return 0

    lax.fori_loop(0, S, clear, 0)

    def gather(i, _):
        for u in range(4):
            n = i * 4 + u
            place, weight = patch_ref[n], weight_ref[n]
            rows = pl.ds(pl.multiple_of(place * CS, CS), CS)
            total[rows, :] = total[rows, :] + weight * in_ref[n].astype(F32)
            share[place] = share[place] + weight
            back_ref[n] = common_ref[place]
        return 0

    lax.fori_loop(0, 2 * S // 4, gather, 0)
    first, last = lanes(CS) == 0, lanes(CS) == S - 1

    def divide(i, _):
        for u in range(4):
            r = i * 4 + u
            rows = pl.ds(pl.multiple_of(r * CS, CS), CS)
            v = (total[rows, :] / jnp.maximum(share[r], 1.0)).astype(BF)
            total[rows, :] = v.astype(F32)
            sea_ref[r] = v
            cols[0] = roll(jnp.where(first, v, cols[0]), -1)
            cols[1] = jnp.where(last, v, roll(cols[1], -1))
        return 0

    lax.fori_loop(0, S // 4, divide, 0)
    es_ref[UP], es_ref[DOWN], es_ref[LEFT], es_ref[RIGHT] = sea_ref[0], sea_ref[S - 1], cols[0], cols[1]
    for quarter in range(1, 4):

        @pl.when(turn == quarter)
        def _():
            for c in range(CS):
                strip = pl.ds(c, S, stride=CS)
                total[strip, :] = turn_matrix(total[strip, :].astype(BF), quarter)
            sea_ref[...] = total[...].reshape(S, CS, S).astype(BF)


def remap(turn, patch, weight, incoming, common):
    sm, vm = pl.BlockSpec(memory_space=SMEM), pl.BlockSpec(memory_space=VMEM)
    shape = jax.ShapeDtypeStruct
    return pl.pallas_call(
        remap_kernel,
        out_shape=(
            shape((S, CS, S), BF),
            shape((4, CS, S), BF),
            shape((2 * S, CS, S), BF),
        ),
        in_specs=[sm] * 3 + [vm] * 2,
        out_specs=(vm,) * 3,
        scratch_shapes=[VMEM((S * CS, S), F32), SMEM((S,), F32), VMEM((2, CS, S), BF)],
        name="remap",
    )(turn, patch, weight, incoming, common)


class Exchange:
    def __init__(self, src, dst, ocean, send, recv, near):
        f, t = lax.axis_index("face"), lax.axis_index("tile")
        n_face, n_tile = lax.axis_size("face"), lax.axis_size("tile")
        fu, fd = (f + n_face - 1) % n_face, (f + 1) % n_face
        tl, tr = (t + n_tile - 1) % n_tile, (t + 1) % n_tile
        copy = lambda n, side, slot, device: pltpu.make_async_remote_copy(
            src_ref=src.at[side],
            dst_ref=dst.at[slot],
            send_sem=send.at[n],
            recv_sem=recv.at[slot],
            device_id=device,
            device_id_type=MESH,
        )
        always, top, bottom = None, f > 0, f < n_face - 1
        if not ocean:
            top = bottom = None
        self.copies = [
            (always, copy(0, LEFT, RIGHT, (f, tl))),
            (always, copy(1, RIGHT, LEFT, (f, tr))),
            (top, copy(2, UP, DOWN, (fu, t))),
            (top, copy(3, UP, DR, (fu, tl))),
            (top, copy(4, UP, DL, (fu, tr))),
            (bottom, copy(5, DOWN, UP, (fd, t))),
            (bottom, copy(6, DOWN, UR, (fd, tl))),
            (bottom, copy(7, DOWN, UL, (fd, tr))),
        ]
        self.local = []
        self.arrivals = [(None, LEFT), (None, RIGHT)]
        if ocean:
            fold = f == n_face - 1
            inner = fold & (lax.rem(t, n_tile // 2) != 0)
            outer = fold & (lax.rem(t, n_tile // 2) != n_tile // 2 - 1)
            left_to, right_to = (2 * n_tile - t) % n_tile, (2 * n_tile - 2 - t) % n_tile
            self.copies += [
                (fold, copy(5, DOWN, DOWN, (f, n_tile - 1 - t))),
                (inner, copy(6, DOWN, DL, (f, left_to))),
                (outer, copy(7, DOWN, DR, (f, right_to))),
            ]
            own_left = fold & (lax.rem(t, n_tile // 2) == 0)
            own_right = fold & (lax.rem(t, n_tile // 2) == n_tile // 2 - 1)
            self.local = [
                (own_left, pltpu.make_async_copy(src.at[DOWN], dst.at[DL], near)),
                (own_right, pltpu.make_async_copy(src.at[DOWN], dst.at[DR], near)),
            ]
            self.arrivals += [(top, UP), (top, UL), (top, UR), (None, DOWN)]
            self.arrivals += [(bottom | inner, DL), (bottom | outer, DR)]
        else:
            self.arrivals += [(None, n) for n in (UP, DOWN, UL, UR, DL, DR)]
        self.arrived = lambda slot: copy(0, LEFT, slot, (f, tl)).wait_recv()

    @staticmethod
    def given(condition, act):
        if condition is None:
            act()
        else:
            pl.when(condition)(act)

    def start(self):
        for condition, each in self.copies + self.local:
            self.given(condition, each.start)

    def wait(self):
        for condition, slot in self.arrivals:
            self.given(condition, partial(self.arrived, slot))
        for condition, each in self.local:
            self.given(condition, each.wait)
        for condition, each in self.copies:
            self.given(condition, each.wait_send)


def place():
    f, t = lax.axis_index("face"), lax.axis_index("tile")
    n_tile = lax.axis_size("tile")
    return f * n_tile + t, lax.axis_size("face") * n_tile, n_tile


def meet_all():
    me, count, n_tile = place()
    barrier = pltpu.get_barrier_semaphore()

    def greet(i, _):
        peer = (me + i) % count
        pl.semaphore_signal(barrier, inc=1, device_id=(peer // n_tile, peer % n_tile), device_id_type=MESH)
        return 0

    lax.fori_loop(1, count, greet, 0)
    pl.semaphore_wait(barrier, count - 1)


def meet_around():
    f, t = lax.axis_index("face"), lax.axis_index("tile")
    n_face, n_tile = lax.axis_size("face"), lax.axis_size("tile")
    barrier = pltpu.get_barrier_semaphore()

    def greet(face, tile):
        pl.semaphore_signal(barrier, inc=1, device_id=(face, tile), device_id_type=MESH)

    for df in (n_face - 1, 0, 1):
        for dt in (n_tile - 1, 0, 1):
            if df or dt:
                greet((f + df) % n_face, (t + dt) % n_tile)
    fold = f == n_face - 1
    half = n_tile // 2
    inner = fold & (lax.rem(t, half) != 0)
    outer = fold & (lax.rem(t, half) != half - 1)
    pl.when(fold)(lambda: greet(f, n_tile - 1 - t))
    pl.when(inner)(lambda: greet(f, (2 * n_tile - t) % n_tile))
    pl.when(outer)(lambda: greet(f, (2 * n_tile - 2 - t) % n_tile))
    more = [jnp.where(condition, 1, 0) for condition in (fold, inner, outer)]
    pl.semaphore_wait(barrier, 8 + more[0] + more[1] + more[2])


def everyone(src, dst, rows, send, recv, near):
    me, count, n_tile = place()

    def copy(peer):
        return pltpu.make_async_remote_copy(
            src_ref=src.at[pl.ds(peer * rows, rows)],
            dst_ref=dst.at[pl.ds(me * rows, rows)],
            send_sem=send,
            recv_sem=recv,
            device_id=(peer // n_tile, peer % n_tile),
            device_id_type=MESH,
        )

    own = pltpu.make_async_copy(src.at[pl.ds(me * rows, rows)], dst.at[pl.ds(me * rows, rows)], near)
    other = (lax.axis_index("face"), (lax.axis_index("tile") + 1) % n_tile)
    rest = pltpu.make_async_remote_copy(
        src_ref=src.at[pl.ds(0, (count - 1) * rows)],
        dst_ref=dst.at[pl.ds(0, (count - 1) * rows)],
        send_sem=send,
        recv_sem=recv,
        device_id=other,
        device_id_type=MESH,
    )

    def start():
        def one(i, _):
            copy((me + i) % count).start()
            return 0

        lax.fori_loop(1, count, one, 0)
        own.start()

    def wait():
        own.wait()
        rest.wait_recv()
        rest.wait_send()

    return start, wait


def first_kernel(pay, meta, ea, eo, pay_in, meta_in, ha, ho, wide, flat, sa, ra, so, ro, near):
    meet_all()
    start_meta, wait_meta = everyone(meta, meta_in, 1, wide.at[0], wide.at[1], near.at[0])
    start_pay, wait_pay = everyone(pay, pay_in, 2, flat.at[0], flat.at[1], near.at[1])
    atmos = Exchange(ea, ha, False, sa, ra, near.at[2])
    ocean = Exchange(eo, ho, True, so, ro, near.at[2])
    start_meta()
    start_pay()
    atmos.start()
    ocean.start()
    wait_meta()
    wait_pay()
    atmos.wait()
    ocean.wait()


DMA = pltpu.SemaphoreType.DMA
EIGHT = [DMA((8,))] * 4


def first_exchange(pay, meta, ea, eo):
    hbm = pl.BlockSpec(memory_space=pl.ANY)
    shape = jax.ShapeDtypeStruct
    return pl.pallas_call(
        first_kernel,
        out_shape=(
            shape(pay.shape, BF),
            shape(meta.shape, F32),
            shape((8, *ea.shape[1:]), BF),
            shape((8, *eo.shape[1:]), BF),
        ),
        in_specs=[hbm] * 4,
        out_specs=(hbm,) * 4,
        scratch_shapes=[DMA((2,)), DMA((2,))] + EIGHT + [DMA((3,))],
        compiler_params=pltpu.CompilerParams(collective_id=0, has_side_effects=True),
        name="first_exchange",
    )(pay, meta, ea, eo)


def second_kernel(slot_ref, back, es, hs, force_ref, hf, got, own, cols, flat, sa, ra, so, ro, near):
    meet_all()
    start_back, wait_back = everyone(back, got, 2, flat.at[0], flat.at[1], near.at[0])
    sea = Exchange(es, hs, False, sa, ra, near.at[1])
    sea.start()
    start_back()
    wait_back()
    first, last = lanes(CS) == 0, lanes(CS) == S - 1

    def put(i, _):
        for u in range(4):
            b = i * 4 + u
            v = got[slot_ref[b]]
            force_ref[b] = v
            cols[0] = roll(jnp.where(first, v, cols[0]), -1)
            cols[1] = jnp.where(last, v, roll(cols[1], -1))
        return 0

    lax.fori_loop(0, S // 4, put, 0)
    own[UP], own[DOWN], own[LEFT], own[RIGHT] = force_ref[0], force_ref[S - 1], cols[0], cols[1]
    sea.wait()
    force = Exchange(own, hf, True, so, ro, near.at[1])
    force.start()
    force.wait()


def second_exchange(slots, back, es):
    hbm, vm, sm = (pl.BlockSpec(memory_space=m) for m in (pl.ANY, VMEM, SMEM))
    shape = jax.ShapeDtypeStruct
    return pl.pallas_call(
        second_kernel,
        out_shape=(
            shape((8, CS, S), BF),
            shape((S, CS, S), BF),
            shape((8, CS, S), BF),
        ),
        in_specs=[sm, hbm, hbm],
        out_specs=(hbm, vm, hbm),
        scratch_shapes=[VMEM((2 * S, CS, S), BF), VMEM((4, CS, S), BF), VMEM((2, CS, S), BF), DMA((2,))]
        + EIGHT
        + [DMA((2,))],
        compiler_params=pltpu.CompilerParams(collective_id=1, has_side_effects=True),
        name="second_exchange",
    )(slots, back, es)


def third_kernel(ea, eo, ha, ho, sa, ra, so, ro, near):
    meet_around()
    atmos = Exchange(ea, ha, False, sa, ra, near)
    ocean = Exchange(eo, ho, True, so, ro, near)
    atmos.start()
    ocean.start()
    atmos.wait()
    ocean.wait()


def third_exchange(ea, eo):
    hbm = pl.BlockSpec(memory_space=pl.ANY)
    shape = jax.ShapeDtypeStruct
    return pl.pallas_call(
        third_kernel,
        out_shape=(
            shape((8, *ea.shape[1:]), BF),
            shape((8, *eo.shape[1:]), BF),
        ),
        in_specs=[hbm] * 2,
        out_specs=(hbm,) * 2,
        scratch_shapes=EIGHT + [DMA],
        compiler_params=pltpu.CompilerParams(collective_id=2, has_side_effects=True),
        name="third_exchange",
    )(ea, eo)


def taps(weight):
    _, outs, channels = weight.shape
    return weight.reshape(3, 3, outs, channels).transpose(0, 2, 1, 3).reshape(3 * outs, 3 * channels)


TURNED_TAPS = (
    (0, 1, 2, 3, 4, 5, 6, 7, 8),
    (2, 5, 8, 1, 4, 7, 0, 3, 6),
    (8, 7, 6, 5, 4, 3, 2, 1, 0),
    (6, 3, 0, 7, 4, 1, 8, 5, 2),
)


def on_device(
    atmos_state, ocean_state, land_mask, face_turns, block_target, block_patch, block_weight,
    atmos_w1, atmos_w2, ocean_w1, ocean_w2,
):
    turn = face_turns.reshape(1)
    face = lax.axis_index("face")
    edge = jnp.where(face == 0, 1, jnp.where(face == lax.axis_size("face") - 1, 2, 0))
    edge = edge.astype(jnp.int32).reshape(1)
    mask = jnp.repeat(land_mask, 32, axis=1).astype(BF)
    order = jnp.array(TURNED_TAPS, jnp.int32)[turn[0]]
    wa1 = taps(jnp.take(atmos_w1, order, axis=0))
    wa2 = taps(jnp.take(atmos_w2, order, axis=0))
    wo1, wo2 = taps(ocean_w1), taps(ocean_w2)
    weight = lax.reduce_precision(block_weight[:, 0], 8, 7)
    xa, xo, ea, eo, pay, meta, common, slots = prepare(
        turn, block_target[:, 0], block_patch[:, 0], weight, atmos_state, ocean_state, mask
    )
    pay_in, meta_in, ha, ho = first_exchange(pay, meta, ea, eo)
    patch_in = meta_in[:, 0, :2].reshape(2 * S).astype(jnp.int32)
    weight_in = meta_in[:, 0, 2:4].reshape(2 * S)
    sea, es, back = remap(turn, patch_in, weight_in, pay_in, common)
    hs, force, hf = second_exchange(slots, back, es)
    hid_a, ea2 = hidden_conv(False, turn, [xa, sea], [ha, hs], wa1, 16)
    hid_o, eo2 = hidden_conv(True, edge, [xo, force], [ho, hf], wo1, 16)
    ha2, ho2 = third_exchange(ea2, eo2)
    atmos_out = out_conv(False, turn, hid_a, ha2, wa2, atmos_state, mask, 8)
    ocean_out = out_conv(True, edge, hid_o, ho2, wo2, ocean_state, mask, 8)
    return atmos_out, ocean_out


def solution(mesh):
    placed = (
        P(None, "face", "tile"),
        P(None, "face", "tile"),
        P("face", "tile"),
        P("face", "tile"),
        P(("face", "tile"), None),
        P(("face", "tile"), None),
        P(("face", "tile"), None),
        P(),
        P(),
        P(),
        P(),
    )
    return jax.shard_map(
        on_device,
        mesh=mesh,
        in_specs=placed,
        out_specs=(P(None, "face", "tile"), P(None, "face", "tile")),
        check_vma=False,
    )
```

profile of v0, /device:TPU:0, one launch (start us, length us, event | category | flops | bytes accessed | tf_op | source)
XLA Modules:
  0.0 201.6 jit_solution(8809633207003915870)
XLA Ops:
  0.6 0.0 copy-start
  1.3 0.7 convert_element_type.10
  2.0 0.7 copy.19.mask_ref
  2.7 1.2 reduce-precision_bitcast_fusion.weight_ref
  3.9 20.1 %prepare.1 = (bf16[128,128,128]{2,1,0:T(8,128)(2,1)}, bf16[128,64,128]{2,1,0:T(8,128)(2,1)}, bf16[4,128,128]{2,1,0:T(8,128)(2,1)}, bf16[4,64,128]{2,1,0:T(8,128)...) custom-call(s32[1]{0:T(128)} %bitcast.36.turn_ref, ...), custom_call_target="tpu_custom_call" | custom-call | tf_op jit(solution)/shard_map/prepare/pallas_call | solution.py:344
  24.1 0.0 copy-start.2
  24.1 0.0 copy-start.4
  24.1 33.3 %first_exchange.1 = (bf16[256,16,128]{2,1,0:T(8,128)(2,1)}, f32[128,1,128]{2,1,0:T(1,128)}, bf16[8,128,128]{2,1,0:T(8,128)(2,1)}, bf16[8,64,128]{2,1,0:T(8,128)(2,1)}) custom-call(bf16[256,16,128]{2,1,0:T(8,128)(2,1)} %get-tuple-element.27.pay, f32[128,1,128]{2,1,0:T(1,128)} %get-tuple-element.28.meta, bf16[4,128,128]{2,1,0:T(8,128)(2,1)} %get-tuple-element.29.ea, ...), custom_call_target="tpu_custom_call" | custom-call | tf_op jit(solution)/shard_map/first_exchange/pallas_call | solution.py:631
  57.4 1.0 convert_reduce_fusion
  58.5 0.7 convert_element_type.13.patch_ref
  59.2 1.1 slice_reduce_fusion
  60.3 0.7 reshape_squeeze.4.weight_ref
  61.0 15.8 %remap.1 = (bf16[128,16,128]{2,1,0:T(8,128)(2,1)}, bf16[4,16,128]{2,1,0:T(8,128)(2,1)}, bf16[256,16,128]{2,1,0:T(8,128)(2,1)}) custom-call(s32[1]{0:T(128)} %bitcast.37.turn_ref, s32[256]{0:T(256)} %convert_element_type.13.patch_ref, f32[256]{0:T(256)} %reshape_squeeze.4.weight_ref, bf16[256,16,128]{2,1,0:T(8,128)(2,1)} %get-tuple-element.32.in_ref, ...), custom_call_target="tpu_custom_call" | custom-call | tf_op jit(solution)/shard_map/remap/pallas_call | solution.py:441
  76.8 39.4 %second_exchange.1 = (bf16[8,16,128]{2,1,0:T(8,128)(2,1)}, bf16[128,16,128]{2,1,0:T(8,128)(2,1)}, bf16[8,16,128]{2,1,0:T(8,128)(2,1)}) custom-call(s32[128]{0:T(128)} %get-tuple-element.36.slot_ref, bf16[256,16,128]{2,1,0:T(8,128)(2,1)} %get-tuple-element.37.back, bf16[4,16,128]{2,1,0:T(8,128)(2,1)} %get-tuple-element.38.es), custom_call_target="tpu_custom_call" | custom-call | tf_op jit(solution)/shard_map/second_exchange/pallas_call | solution.py:676
  116.2 0.0 copy-done.2
  116.3 0.1 copy.39
  116.4 0.8 reshape.77.refs_4_
  117.2 11.3 %hidden_ocean.1 = (bf16[128,64,128]{2,1,0:T(8,128)(2,1)}, bf16[4,64,128]{2,1,0:T(8,128)(2,1)}) custom-call(s32[1]{0:T(128)} %bitcast.10.mode_ref, bf16[128,64,128]{2,1,0:T(8,128)(2,1)} %get-tuple-element.42.refs_0_, bf16[128,16,128]{2,1,0:T(8,128)(2,1)} %get-tuple-element.43.refs_1_, bf16[8,64,128]{2,1,0:T(8,128)(2,1)} %get-tuple-element.44.refs_2_, ...), custom_call_target="tpu_custom_call" | custom-call | tf_op jit(solution)/shard_map/hidden_ocean/pallas_call | solution.py:199
  128.5 0.0 copy-done.4
  128.5 0.0 copy-done
  128.5 0.6 gather_fusion
  129.2 0.0 copy-start.3
  129.2 0.1 squeeze.14
  129.3 0.1 copy.20
  129.4 0.3 copy_select_fusion
  129.7 0.1 copy.36
  129.7 0.9 copy.22.refs_4_
  130.7 21.0 %hidden_atmos.1 = (bf16[128,128,128]{2,1,0:T(8,128)(2,1)}, bf16[4,128,128]{2,1,0:T(8,128)(2,1)}) custom-call(s32[1]{0:T(128)} %bitcast.38.mode_ref, bf16[128,128,128]{2,1,0:T(8,128)(2,1)} %get-tuple-element.26.refs_0_, bf16[128,16,128]{2,1,0:T(8,128)(2,1)} %get-tuple-element.34.refs_1_, bf16[8,128,128]{2,1,0:T(8,128)(2,1)} %get-tuple-element.35.refs_2_, ...), custom_call_target="tpu_custom_call" | custom-call | tf_op jit(solution)/shard_map/hidden_atmos/pallas_call | solution.py:199
  151.7 0.0 copy-start.1
  151.7 12.0 %third_exchange.1 = (bf16[8,128,128]{2,1,0:T(8,128)(2,1)}, bf16[8,64,128]{2,1,0:T(8,128)(2,1)}) custom-call(bf16[4,128,128]{2,1,0:T(8,128)(2,1)} %get-tuple-element.41.ea, bf16[4,64,128]{2,1,0:T(8,128)(2,1)} %get-tuple-element.46.eo), custom_call_target="tpu_custom_call" | custom-call | tf_op jit(solution)/shard_map/third_exchange/pallas_call | solution.py:706
  163.7 0.0 copy-done.3
  163.7 0.1 copy.38
  163.8 0.8 reshape.80.w_ref
  164.6 12.9 %out_ocean.1 = bf16[64,128,128]{2,1,0:T(8,128)(2,1)} custom-call(s32[1]{0:T(128)} %bitcast.10.mode_ref, bf16[128,64,128]{2,1,0:T(8,128)(2,1)} %get-tuple-element.48.hid_ref, bf16[8,64,128]{2,1,0:T(8,128)(2,1)} %get-tuple-element.49.halo_ref, bf16[192,192]{1,0:T(8,128)(2,1)} %reshape.80.w_ref, bf16[64,128,128]{2,1,0:T(8,128)(2,1)} %base_ref.3, ...), custom_call_target="tpu_custom_call" | custom-call | tf_op jit(solution)/shard_map/out_ocean/pallas_call | solution.py:244
  177.5 0.0 copy-done.1
  177.5 0.6 gather_fusion.1
  178.2 0.3 copy_select_fusion.1
  178.5 0.7 copy.37
  179.2 22.4 %out_atmos.1 = bf16[128,128,128]{2,1,0:T(8,128)(2,1)} custom-call(s32[1]{0:T(128)} %bitcast.39.mode_ref, bf16[128,128,128]{2,1,0:T(8,128)(2,1)} %get-tuple-element.40.hid_ref, bf16[8,128,128]{2,1,0:T(8,128)(2,1)} %get-tuple-element.47.halo_ref, bf16[384,384]{1,0:T(8,128)(2,1)} %bitcast.47, bf16[128,128,128]{2,1,0:T(8,128)(2,1)} %base_ref.2, ...), custom_call_target="tpu_custom_call" | custom-call | tf_op jit(solution)/shard_map/out_atmos/pallas_call | solution.py:244
  (5 shorter events, 0.1 us)
Async XLA Ops:
  0.6 127.9 %copy-start = (bf16[9,128,144]{1,2,0:T(8,128)(2,1)S(1)}, bf16[9,128,144]{1,2,0:T(8,128)(2,1)}, u32[]{:S(2)}) copy-start(bf16[9,128,144]{1,2,0:T(8,128)(2,1)} %param.19) | copy-start | bytes 995332
  24.1 92.2 %copy-start.2 = (bf16[9,64,80]{2,1,0:T(8,128)(2,1)S(1)}, bf16[9,64,80]{2,1,0:T(8,128)(2,1)}, u32[]{:S(2)}) copy-start(bf16[9,64,80]{2,1,0:T(8,128)(2,1)} %param.21) | copy-start | bytes 276484
  24.1 104.4 %copy-start.4 = (s32[4,9]{1,0:T(4,128)S(1)}, s32[4,9]{1,0:T(4,128)}, u32[]{:S(2)}) copy-start(s32[4,9]{1,0:T(4,128)} %constant.45.clone) | copy-start | bytes 436
  129.2 34.5 %copy-start.3 = (bf16[9,64,64]{2,1,0:T(8,128)(2,1)S(1)}, bf16[9,64,64]{2,1,0:T(8,128)(2,1)}, u32[]{:S(2)}) copy-start(bf16[9,64,64]{2,1,0:T(8,128)(2,1)} %param.22) | copy-start | bytes 221188
  151.7 25.9 %copy-start.1 = (bf16[9,128,128]{2,1,0:T(8,128)(2,1)S(1)}, bf16[9,128,128]{2,1,0:T(8,128)(2,1)}, u32[]{:S(2)}) copy-start(bf16[9,128,128]{2,1,0:T(8,128)(2,1)} %param.20) | copy-start | bytes 884740
where the time goes:
time: 202 us
  Pallas kernels  188 us (93%)
  local copies, waits for them, and re-layouts  8.33 us (4%)
  other arithmetic  3.51 us (2%)
    pallas_call x1, Pallas kernels, second_exchange(): pl.pallas_call(second_kernel, out_shape=(shape((8, CS, S), BF), shape((S,...  39.4 us
    pallas_call x2, Pallas kernels, out_conv(): pl.pallas_call(partial(out_kernel, ocean, unroll), out_shape=jax.ShapeDty...  35.3 us
    pallas_call x1, Pallas kernels, first_exchange(): pl.pallas_call(first_kernel, out_shape=(shape(pay.shape, BF), shape(meta....  33.3 us
    pallas_call x2, Pallas kernels, hidden_conv(): pl.pallas_call(partial(hidden_kernel, ocean, unroll, count), out_shape=(j...  32.3 us
    pallas_call x1, Pallas kernels, prepare(): pl.pallas_call(prep_kernel, grid=(8,), out_shape=(shape((S, ca, S), BF),...  20.1 us
    pallas_call x1, Pallas kernels, remap(): pl.pallas_call(remap_kernel, out_shape=(shape((S, CS, S), BF), shape((4,...  15.8 us
    pallas_call x1, Pallas kernels, third_exchange(): pl.pallas_call(third_kernel, out_shape=(shape((8, *ea.shape[1:]), BF), sh...  12 us

commit v1 on v0

--- a/solution.py
+++ b/solution.py
@@ -90,6 +90,42 @@
     def _():
         for i in (DOWN, DL, DR):
             target[i] = reversed_lanes(source[i])
+
+
+def blended_sides(table, mode, source, flipped, target):
+    count, channels = source.shape[0], source.shape[1]
+    flat = source[...].reshape(count * channels, S)
+    flipped[:count] = reversed_lanes(flat).reshape(count, channels, S)
+    for i, row in enumerate(table):
+        v = None
+        for turn, (side, flip) in enumerate(row):
+            each = flipped[side] if flip else source[side]
+            v = each if v is None else jnp.where(mode == turn, each, v)
+        target[i] = v
+
+
+def folded_sides(source, target):
+    f, n_face = lax.axis_index("face"), lax.axis_size("face")
+    target[LEFT], target[RIGHT] = source[LEFT], source[RIGHT]
+    for i in (UP, UL, UR):
+
+        @pl.when(f == 0)
+        def _():
+            target[i] = jnp.zeros(target.shape[1:], BF)
+
+        @pl.when(f > 0)
+        def _():
+            target[i] = source[i]
+
+    for i in (DOWN, DL, DR):
+
+        @pl.when(f == n_face - 1)
+        def _():
+            target[i] = reversed_lanes(source[i])
+
+        @pl.when(f < n_face - 1)
+        def _():
+            target[i] = source[i]
 
 
 def turn_matrix(v, turns):
@@ -156,19 +192,7 @@
     lax.fori_loop(0, 4, sixteen, 0)
 
 
-def hidden_kernel(ocean, unroll, count, mode_ref, *refs):
-    parts, refs = refs[:count], refs[count:]
-    halos, refs = refs[:count], refs[count:]
-    w_ref, hid_ref, edge_ref, refs = refs[0], refs[1], refs[2], refs[3:]
-    sides, refs = refs[:count], refs[count:]
-    runs, refs = refs[:count], refs[count:]
-    carry, cols, own = refs
-    mode = mode_ref[0]
-    for halo, side in zip(halos, sides):
-        if ocean:
-            ocean_sides(mode, halo, side)
-        else:
-            select_sides(TO_STORED, mode, halo, side)
+def hidden_rows(parts, sides, runs, w_ref, hid_ref, carry, cols, own, unroll):
     outs = hid_ref.shape[1]
     first, last = lanes(outs) == 0, lanes(outs) == S - 1
 
@@ -184,31 +208,6 @@
     own[UP], own[DOWN] = hid_ref[0], hid_ref[S - 1]
     own[LEFT] = jnp.where(upper, cols[1], roll(cols[0], 64))
     own[RIGHT] = jnp.where(upper, cols[3], roll(cols[2], 64))
-    if ocean:
-        for i in range(4):
-            edge_ref[i] = own[i]
-    else:
-        select_sides(TO_COMMON, mode, own, edge_ref)
-
-
-def hidden_conv(ocean, mode, parts, halos, weight, unroll):
-    outs = weight.shape[0] // 3
-    count = len(parts)
-    channels = [p.shape[1] for p in parts]
-    vm = pl.BlockSpec(memory_space=VMEM)
-    return pl.pallas_call(
-        partial(hidden_kernel, ocean, unroll, count),
-        out_shape=(
-            jax.ShapeDtypeStruct((S, outs, S), BF),
-            jax.ShapeDtypeStruct((4, outs, S), BF),
-        ),
-        in_specs=[pl.BlockSpec(memory_space=SMEM)] + [vm] * (2 * count + 1),
-        out_specs=(vm, vm),
-        scratch_shapes=[VMEM((8, c, S), BF) for c in channels]
-        + [VMEM((4, c, S), BF) for c in channels]
-        + [VMEM((2, outs, 2 * S), F32), VMEM((4, outs, S), BF), VMEM((4, outs, S), BF)],
-        name="hidden_ocean" if ocean else "hidden_atmos",
-    )(mode, *parts, *halos, weight)
 
 
 def out_kernel(ocean, unroll, mode_ref, hid_ref, halo_ref, w_ref, base_ref, mask_ref, out_ref, side, run, carry, stage):
@@ -257,174 +256,93 @@
 
 
 def prep_kernel(
-    turn_ref, target_ref, patch_ref, weight_ref, atmos_ref, surface_ref, ocean_ref, mask_ref,
-    xa_ref, xo_ref, ea_ref, eo_ref, pay_ref, meta_ref, common_ref, slot_ref,
-    wide_a, wide_o, wide_s, cols_a, cols_o, own, surf, tally, patch_of, weight_of,
+    turn_ref, target_ref, patch_ref, weight_ref, atmos_ref, ocean_ref, mask_ref,
+    pay_ref, meta_ref, common_ref, slot_ref, surf, tally,
 ):
-    step = pl.program_id(0)
     turn = turn_ref[0]
-
-    def columns(cols, v):
-        first, last = lanes(v.shape[0]) == 0, lanes(v.shape[0]) == S - 1
-        cols[0] = roll(jnp.where(first, v, cols[0]), -1)
-        cols[1] = jnp.where(last, v, roll(cols[1], -1))
-
-    @pl.when(step == 0)
-    def _():
-        pay_ref[...] = jnp.zeros_like(pay_ref)
-
-        def clear(p, _):
-            tally[p] = 0
-            for n in range(2):
-                patch_of[2 * p + n] = 0
-                weight_of[2 * p + n] = 0.0
-            return 0
-
-        lax.fori_loop(0, S, clear, 0)
-
-    wide_a[...] = atmos_ref[...].astype(F32).reshape(wide_a.shape)
     gate = mask_ref[...].astype(F32)[None]
-    wide_o[...] = (ocean_ref[...].astype(F32) * gate).reshape(wide_o.shape)
-    for y in range(16):
-        v = wide_a[pl.ds(y, S, stride=16), :].astype(BF)
-        xa_ref[y] = v
-        columns(cols_a, v)
-        v = wide_o[pl.ds(y, eo_ref.shape[1], stride=16), :].astype(BF)
-        xo_ref[y] = v
-        columns(cols_o, v)
-        surf[step * 16 + y] = v[:CS]
-
-    @pl.when(step == 0)
-    def _():
-        own[UP] = xa_ref[0]
-        eo_ref[UP] = xo_ref[0]
-
-    @pl.when(step == 7)
-    def _():
-        own[DOWN], own[LEFT], own[RIGHT] = xa_ref[15], cols_a[0], cols_a[1]
-        eo_ref[DOWN], eo_ref[LEFT], eo_ref[RIGHT] = xo_ref[15], cols_o[0], cols_o[1]
-        select_sides(TO_COMMON, turn, own, ea_ref)
-
-        def place(b, _):
+    surf[...] = jnp.swapaxes((ocean_ref[...].astype(F32) * gate).astype(BF), 0, 1)
+    pay_ref[...] = jnp.zeros_like(pay_ref)
+    meta_ref[...] = jnp.zeros_like(meta_ref)
+
+    def clear(i, _):
+        for u in range(8):
+            tally[i * 8 + u] = 0
+        return 0
+
+    lax.fori_loop(0, S // 8, clear, 0)
+    lane = lanes(1)
+
+    def place(i, _):
+        for u in range(4):
+            b = i * 4 + u
             goal = target_ref[b]
             seen = tally[goal]
             slot = 2 * goal + seen
             tally[goal] = seen + 1
             slot_ref[b] = slot
             pay_ref[slot] = surf[b]
-            patch_of[slot] = patch_ref[b]
-            weight_of[slot] = weight_ref[b]
-            return 0
-
-        lax.fori_loop(0, S, place, 0)
-        lane = lanes(1)
-
-        def describe(p, _):
-            places = jnp.where(lane == 0, patch_of[2 * p], patch_of[2 * p + 1]).astype(F32)
-            shares = jnp.where(lane == 2, weight_of[2 * p], weight_of[2 * p + 1])
-            meta_ref[p] = jnp.where(lane < 2, places, shares)
-            return 0
-
-        lax.fori_loop(0, S, describe, 0)
-        for quarter in range(4):
-
-            @pl.when(turn == quarter)
-            def _():
-                for c in range(CS):
-                    wide_s[pl.ds(c, S, stride=CS), :] = turn_matrix(surface_ref[c], (4 - quarter) % 4)
-
-        common_ref[...] = wide_s[...].reshape(S, CS, S).astype(BF)
+            spot = jnp.full((1, S), patch_ref[b], jnp.int32).astype(F32)
+            meta_ref[slot] = jnp.where(lane == 0, spot, weight_ref[b])
+        return 0
+
+    lax.fori_loop(0, S // 4, place, 0)
+    for quarter in range(4):
+
+        @pl.when(turn == quarter)
+        def _():
+            for c in range(CS):
+                common_ref[c] = turn_matrix(atmos_ref[c], (4 - quarter) % 4).astype(BF)
 
 
 def prepare(turn, target, patch, weight, atmos, ocean, mask):
-    ca, co = atmos.shape[0], ocean.shape[0]
     sm = pl.BlockSpec(memory_space=SMEM)
+    head = pl.BlockSpec((CS, S, S), lambda i: (0, 0, 0))
     whole = lambda shape: pl.BlockSpec(shape, lambda i: (0,) * len(shape))
     shape = jax.ShapeDtypeStruct
     return pl.pallas_call(
         prep_kernel,
-        grid=(8,),
+        grid=(1,),
         out_shape=(
-            shape((S, ca, S), BF),
-            shape((S, co, S), BF),
-            shape((4, ca, S), BF),
-            shape((4, co, S), BF),
             shape((2 * S, CS, S), BF),
-            shape((S, 1, S), F32),
-            shape((S, CS, S), BF),
+            shape((2 * S, 1, S), F32),
+            shape((CS, S, S), BF),
             shape((S,), jnp.int32),
         ),
-        in_specs=[sm] * 4
-        + [
-            pl.BlockSpec((ca, 16, S), lambda i: (0, i, 0)),
-            whole((CS, S, S)),
-            pl.BlockSpec((co, 16, S), lambda i: (0, i, 0)),
-            pl.BlockSpec((16, S), lambda i: (i, 0)),
-        ],
-        out_specs=(
-            pl.BlockSpec((16, ca, S), lambda i: (i, 0, 0)),
-            pl.BlockSpec((16, co, S), lambda i: (i, 0, 0)),
-            whole((4, ca, S)),
-            whole((4, co, S)),
-            whole((2 * S, CS, S)),
-            whole((S, 1, S)),
-            whole((S, CS, S)),
-            sm,
-        ),
-        scratch_shapes=[
-            VMEM((ca * 16, S), F32),
-            VMEM((co * 16, S), F32),
-            VMEM((S * CS, S), F32),
-            VMEM((2, ca, S), BF),
-            VMEM((2, co, S), BF),
-            VMEM((4, ca, S), BF),
-            VMEM((S, CS, S), BF),
-            SMEM((S,), jnp.int32),
-            SMEM((2 * S,), jnp.int32),
-            SMEM((2 * S,), F32),
-        ],
+        in_specs=[sm] * 4 + [head, head, whole((S, S))],
+        out_specs=(whole((2 * S, CS, S)), whole((2 * S, 1, S)), whole((CS, S, S)), sm),
+        scratch_shapes=[VMEM((S, CS, S), BF), SMEM((S,), jnp.int32)],
         name="prepare",
-    )(turn, target, patch, weight, atmos, atmos, ocean, mask)
+    )(turn, target, patch, weight, atmos, ocean, mask)
 
 
 def remap_kernel(
-    turn_ref, patch_ref, weight_ref, in_ref, common_ref, sea_ref, es_ref, back_ref, total, share, cols
+    turn_ref, meta_ref, in_ref, common_ref, sea_ref, es_ref, back_ref, wide, total, spread
 ):
     turn = turn_ref[0]
-    total[...] = jnp.zeros_like(total)
-
-    def clear(p, _):
-        share[p] = 0.0
-        return 0
-
-    lax.fori_loop(0, S, clear, 0)
-
-    def gather(i, _):
-        for u in range(4):
-            n = i * 4 + u
-            place, weight = patch_ref[n], weight_ref[n]
-            rows = pl.ds(pl.multiple_of(place * CS, CS), CS)
-            total[rows, :] = total[rows, :] + weight * in_ref[n].astype(F32)
-            share[place] = share[place] + weight
-            back_ref[n] = common_ref[place]
-        return 0
-
-    lax.fori_loop(0, 2 * S // 4, gather, 0)
-    first, last = lanes(CS) == 0, lanes(CS) == S - 1
-
-    def divide(i, _):
-        for u in range(4):
-            r = i * 4 + u
-            rows = pl.ds(pl.multiple_of(r * CS, CS), CS)
-            v = (total[rows, :] / jnp.maximum(share[r], 1.0)).astype(BF)
-            total[rows, :] = v.astype(F32)
-            sea_ref[r] = v
-            cols[0] = roll(jnp.where(first, v, cols[0]), -1)
-            cols[1] = jnp.where(last, v, roll(cols[1], -1))
-        return 0
-
-    lax.fori_loop(0, S // 4, divide, 0)
-    es_ref[UP], es_ref[DOWN], es_ref[LEFT], es_ref[RIGHT] = sea_ref[0], sea_ref[S - 1], cols[0], cols[1]
+    meta = meta_ref[...].reshape(2 * S, S)
+    spot = jnp.broadcast_to(meta[:, 0:1], (2 * S, S))
+    share = jnp.broadcast_to(meta[:, 1:2], (2 * S, S))
+    faces = spot == lax.broadcasted_iota(jnp.int32, (2 * S, S), 1).astype(F32)
+    pick = jnp.where(faces, 1.0, 0.0).astype(BF)
+    spread[...] = dot_nt(eye(), jnp.where(faces, share, 0.0).astype(BF)).astype(BF)
+    amount = jnp.maximum(dot(spread[...], jnp.ones((2 * S, S), BF)), 1.0)
+    wide[...] = in_ref[...].astype(F32).reshape(wide.shape)
+    sides = lax.broadcasted_iota(jnp.int32, (16, S), 0)
+    along = lax.broadcasted_iota(jnp.int32, (16, S), 1)
+    ends = jnp.where(along == jnp.where(sides < 2, sides * (S - 1), -1), 1.0, 0.0).astype(BF)
+    for c in range(CS):
+        strip = pl.ds(c, 2 * S, stride=CS)
+        blocks = wide[strip, :].astype(BF)
+        v = (dot(spread[...], blocks) / amount).astype(BF)
+        wide[strip, :] = dot(pick, common_ref[c])
+        total[pl.ds(c, S, stride=CS), :] = v.astype(F32)
+        edge = dot_nt(ends, v)
+        es_ref[LEFT, pl.ds(c, 1), :] = edge[0:1]
+        es_ref[RIGHT, pl.ds(c, 1), :] = edge[1:2]
+    back_ref[...] = wide[...].reshape(2 * S, CS, S).astype(BF)
+    es_ref[UP] = total[pl.ds(0, CS), :]
+    es_ref[DOWN] = total[pl.ds((S - 1) * CS, CS), :]
     for quarter in range(1, 4):
 
         @pl.when(turn == quarter)
@@ -432,24 +350,25 @@
             for c in range(CS):
                 strip = pl.ds(c, S, stride=CS)
                 total[strip, :] = turn_matrix(total[strip, :].astype(BF), quarter)
-            sea_ref[...] = total[...].reshape(S, CS, S).astype(BF)
-
-
-def remap(turn, patch, weight, incoming, common):
+
+    sea_ref[...] = total[...].reshape(S, CS, S).astype(BF)
+
+
+def remap(turn, meta, incoming, common):
     sm, vm = pl.BlockSpec(memory_space=SMEM), pl.BlockSpec(memory_space=VMEM)
     shape = jax.ShapeDtypeStruct
     return pl.pallas_call(
         remap_kernel,
         out_shape=(
             shape((S, CS, S), BF),
-            shape((4, CS, S), BF),
+            shape((4, CS, S), F32),
             shape((2 * S, CS, S), BF),
         ),
-        in_specs=[sm] * 3 + [vm] * 2,
+        in_specs=[sm] + [vm] * 3,
         out_specs=(vm,) * 3,
-        scratch_shapes=[VMEM((S * CS, S), F32), SMEM((S,), F32), VMEM((2, CS, S), BF)],
+        scratch_shapes=[VMEM((2 * S * CS, S), F32), VMEM((S * CS, S), F32), VMEM((S, 2 * S), BF)],
         name="remap",
-    )(turn, patch, weight, incoming, common)
+    )(turn, meta, incoming, common)
 
 
 class Exchange:
@@ -542,29 +461,6 @@
     pl.semaphore_wait(barrier, count - 1)
 
 
-def meet_around():
-    f, t = lax.axis_index("face"), lax.axis_index("tile")
-    n_face, n_tile = lax.axis_size("face"), lax.axis_size("tile")
-    barrier = pltpu.get_barrier_semaphore()
-
-    def greet(face, tile):
-        pl.semaphore_signal(barrier, inc=1, device_id=(face, tile), device_id_type=MESH)
-
-    for df in (n_face - 1, 0, 1):
-        for dt in (n_tile - 1, 0, 1):
-            if df or dt:
-                greet((f + df) % n_face, (t + dt) % n_tile)
-    fold = f == n_face - 1
-    half = n_tile // 2
-    inner = fold & (lax.rem(t, half) != 0)
-    outer = fold & (lax.rem(t, half) != half - 1)
-    pl.when(fold)(lambda: greet(f, n_tile - 1 - t))
-    pl.when(inner)(lambda: greet(f, (2 * n_tile - t) % n_tile))
-    pl.when(outer)(lambda: greet(f, (2 * n_tile - 2 - t) % n_tile))
-    more = [jnp.where(condition, 1, 0) for condition in (fold, inner, outer)]
-    pl.semaphore_wait(barrier, 8 + more[0] + more[1] + more[2])
-
-
 def everyone(src, dst, rows, send, recv, near):
     me, count, n_tile = place()
 
@@ -605,51 +501,134 @@
     return start, wait
 
 
-def first_kernel(pay, meta, ea, eo, pay_in, meta_in, ha, ho, wide, flat, sa, ra, so, ro, near):
+DMA = pltpu.SemaphoreType.DMA
+EIGHT = [DMA((8,))] * 4
+
+
+def first_kernel(
+    turn_ref, mask_ref, pay, meta, atmos, ocean, pay_in, meta_in, xa_ref, xo_ref, ha, ho,
+    held_a, held_o, wide_a, wide_o, cols_a, cols_o, own_a, flip_a, side_a, own_o,
+    loads, wide, flat, sa, ra, so, ro, near,
+):
+    def load(g, n):
+        source, held = ((atmos, held_a), (ocean, held_o))[n]
+        rows = pl.ds(pl.multiple_of(g * 16, 16), 16)
+        return pltpu.make_async_copy(source.at[:, rows, :], held.at[g], loads.at[n, g])
+
+    for n in range(2):
+        for g in range(8):
+            load(g, n).start()
     meet_all()
-    start_meta, wait_meta = everyone(meta, meta_in, 1, wide.at[0], wide.at[1], near.at[0])
+    start_meta, wait_meta = everyone(meta, meta_in, 2, wide.at[0], wide.at[1], near.at[0])
     start_pay, wait_pay = everyone(pay, pay_in, 2, flat.at[0], flat.at[1], near.at[1])
-    atmos = Exchange(ea, ha, False, sa, ra, near.at[2])
-    ocean = Exchange(eo, ho, True, so, ro, near.at[2])
     start_meta()
     start_pay()
-    atmos.start()
-    ocean.start()
+
+    def columns(cols, v):
+        first, last = lanes(v.shape[0]) == 0, lanes(v.shape[0]) == S - 1
+        cols[0] = roll(jnp.where(first, v, cols[0]), -1)
+        cols[1] = jnp.where(last, v, roll(cols[1], -1))
+
+    def sixteen(g, _):
+        for n in range(2):
+            load(g, n).wait()
+        rows = pl.ds(pl.multiple_of(g * 16, 16), 16)
+        wide_a[...] = held_a[g].astype(F32).reshape(wide_a.shape)
+        gate = mask_ref[rows, :].astype(F32)[None]
+        wide_o[...] = (held_o[g].astype(F32) * gate).reshape(wide_o.shape)
+        for y in range(16):
+            v = wide_a[pl.ds(y, wide_a.shape[0] // 16, stride=16), :].astype(BF)
+            xa_ref[g * 16 + y] = v
+            columns(cols_a, v)
+            v = wide_o[pl.ds(y, wide_o.shape[0] // 16, stride=16), :].astype(BF)
+            xo_ref[g * 16 + y] = v
+            columns(cols_o, v)
+        return 0
+
+    cols_a[...] = jnp.zeros_like(cols_a)
+    cols_o[...] = jnp.zeros_like(cols_o)
+    lax.fori_loop(0, 8, sixteen, 0)
+    own_a[UP], own_a[DOWN], own_a[LEFT], own_a[RIGHT] = xa_ref[0], xa_ref[S - 1], cols_a[0], cols_a[1]
+    own_o[UP], own_o[DOWN], own_o[LEFT], own_o[RIGHT] = xo_ref[0], xo_ref[S - 1], cols_o[0], cols_o[1]
+    blended_sides(TO_COMMON, turn_ref[0], own_a, flip_a, side_a)
+    at = Exchange(side_a, ha, False, sa, ra, near.at[2])
+    oc = Exchange(own_o, ho, True, so, ro, near.at[2])
+    at.start()
+    oc.start()
     wait_meta()
     wait_pay()
-    atmos.wait()
-    ocean.wait()
-
-
-DMA = pltpu.SemaphoreType.DMA
-EIGHT = [DMA((8,))] * 4
-
-
-def first_exchange(pay, meta, ea, eo):
-    hbm = pl.BlockSpec(memory_space=pl.ANY)
+    at.wait()
+    oc.wait()
+
+
+def first_exchange(turn, mask, pay, meta, atmos, ocean):
+    hbm, vm, sm = (pl.BlockSpec(memory_space=m) for m in (pl.ANY, VMEM, SMEM))
     shape = jax.ShapeDtypeStruct
+    ca, co = atmos.shape[0], ocean.shape[0]
     return pl.pallas_call(
         first_kernel,
         out_shape=(
             shape(pay.shape, BF),
             shape(meta.shape, F32),
-            shape((8, *ea.shape[1:]), BF),
-            shape((8, *eo.shape[1:]), BF),
+            shape((S, ca, S), BF),
+            shape((S, co, S), BF),
+            shape((8, ca, S), BF),
+            shape((8, co, S), BF),
         ),
-        in_specs=[hbm] * 4,
-        out_specs=(hbm,) * 4,
-        scratch_shapes=[DMA((2,)), DMA((2,))] + EIGHT + [DMA((3,))],
+        in_specs=[sm, vm] + [hbm] * 4,
+        out_specs=(hbm, hbm, vm, vm, hbm, hbm),
+        scratch_shapes=[
+            VMEM((8, ca, 16, S), BF),
+            VMEM((8, co, 16, S), BF),
+            VMEM((ca * 16, S), F32),
+            VMEM((co * 16, S), F32),
+            VMEM((2, ca, S), BF),
+            VMEM((2, co, S), BF),
+            VMEM((4, ca, S), BF),
+            VMEM((4, ca, S), BF),
+            VMEM((4, ca, S), BF),
+            VMEM((4, co, S), BF),
+            DMA((2, 8)),
+            DMA((2,)),
+            DMA((2,)),
+        ]
+        + EIGHT
+        + [DMA((3,))],
         compiler_params=pltpu.CompilerParams(collective_id=0, has_side_effects=True),
         name="first_exchange",
-    )(pay, meta, ea, eo)
-
-
-def second_kernel(slot_ref, back, es, hs, force_ref, hf, got, own, cols, flat, sa, ra, so, ro, near):
+    )(turn, mask, pay, meta, atmos, ocean)
+
+
+def second_kernel(
+    unroll, slot_ref, turn_ref, back, es, xa, xo, sea_ref, ha_ref, ho_ref, wa_ref, wo_ref,
+    hid_a, hid_o, ha2, ho2,
+    x_a, x_o, hs, hf, got, force, flip, flip_s, sides_a, sides_s, sides_o, sides_f,
+    run_a, run_s, run_o, run_f, carry_a, carry_o, cols_a, cols_o, cols_f, own_a, out_a, own_o, own_f,
+    loads, flat, sem_s, sem_f, sem_a, sem_o, near,
+):
+    turn = turn_ref[0]
+    load_a = pltpu.make_async_copy(xa, x_a, loads.at[0])
+    load_o = pltpu.make_async_copy(xo, x_o, loads.at[1])
+    load_a.start()
+    load_o.start()
     meet_all()
     start_back, wait_back = everyone(back, got, 2, flat.at[0], flat.at[1], near.at[0])
-    sea = Exchange(es, hs, False, sa, ra, near.at[1])
+    sea = Exchange(es, hs, False, sem_s.at[0], sem_s.at[1], near.at[1])
     sea.start()
     start_back()
+    blended_sides(TO_STORED, turn, ha_ref, flip, sides_a)
+    folded_sides(ho_ref, sides_o)
+    load_a.wait()
+    sea.wait()
+    blended_sides(TO_STORED, turn, hs, flip_s, sides_s)
+    cols_a[...] = jnp.zeros_like(cols_a)
+    cols_o[...] = jnp.zeros_like(cols_o)
+    cols_f[...] = jnp.zeros_like(cols_f)
+    hidden_rows([x_a, sea_ref], [sides_a, sides_s], [run_a, run_s], wa_ref, hid_a, carry_a, cols_a, own_a, unroll)
+    blended_sides(TO_COMMON, turn, own_a, flip, out_a)
+    atmos = Exchange(out_a, ha2, False, sem_a.at[0], sem_a.at[1], near.at[1])
+    atmos.start()
+    load_o.wait()
     wait_back()
     first, last = lanes(CS) == 0, lanes(CS) == S - 1
 
@@ -657,64 +636,52 @@
         for u in range(4):
             b = i * 4 + u
             v = got[slot_ref[b]]
-            force_ref[b] = v
-            cols[0] = roll(jnp.where(first, v, cols[0]), -1)
-            cols[1] = jnp.where(last, v, roll(cols[1], -1))
+            force[b] = v
+            cols_f[0] = roll(jnp.where(first, v, cols_f[0]), -1)
+            cols_f[1] = jnp.where(last, v, roll(cols_f[1], -1))
         return 0
 
     lax.fori_loop(0, S // 4, put, 0)
-    own[UP], own[DOWN], own[LEFT], own[RIGHT] = force_ref[0], force_ref[S - 1], cols[0], cols[1]
-    sea.wait()
-    force = Exchange(own, hf, True, so, ro, near.at[1])
-    force.start()
-    force.wait()
-
-
-def second_exchange(slots, back, es):
-    hbm, vm, sm = (pl.BlockSpec(memory_space=m) for m in (pl.ANY, VMEM, SMEM))
-    shape = jax.ShapeDtypeStruct
-    return pl.pallas_call(
-        second_kernel,
-        out_shape=(
-            shape((8, CS, S), BF),
-            shape((S, CS, S), BF),
-            shape((8, CS, S), BF),
-        ),
-        in_specs=[sm, hbm, hbm],
-        out_specs=(hbm, vm, hbm),
-        scratch_shapes=[VMEM((2 * S, CS, S), BF), VMEM((4, CS, S), BF), VMEM((2, CS, S), BF), DMA((2,))]
-        + EIGHT
-        + [DMA((2,))],
-        compiler_params=pltpu.CompilerParams(collective_id=1, has_side_effects=True),
-        name="second_exchange",
-    )(slots, back, es)
-
-
-def third_kernel(ea, eo, ha, ho, sa, ra, so, ro, near):
-    meet_around()
-    atmos = Exchange(ea, ha, False, sa, ra, near)
-    ocean = Exchange(eo, ho, True, so, ro, near)
-    atmos.start()
+    own_f[UP], own_f[DOWN], own_f[LEFT], own_f[RIGHT] = force[0], force[S - 1], cols_f[0], cols_f[1]
+    forcing = Exchange(own_f, hf, True, sem_f.at[0], sem_f.at[1], near.at[2])
+    forcing.start()
+    forcing.wait()
+    folded_sides(hf, sides_f)
+    hidden_rows([x_o, force], [sides_o, sides_f], [run_o, run_f], wo_ref, hid_o, carry_o, cols_o, own_o, unroll)
+    ocean = Exchange(own_o, ho2, True, sem_o.at[0], sem_o.at[1], near.at[2])
     ocean.start()
     atmos.wait()
     ocean.wait()
 
 
-def third_exchange(ea, eo):
-    hbm = pl.BlockSpec(memory_space=pl.ANY)
+def second_exchange(slots, turn, back, es, xa, xo, sea, ha, ho, wa, wo, unroll):
+    hbm, vm, sm = (pl.BlockSpec(memory_space=m) for m in (pl.ANY, VMEM, SMEM))
     shape = jax.ShapeDtypeStruct
+    ca, co = xa.shape[1], xo.shape[1]
+    bf = lambda *dims: VMEM(dims, BF)
     return pl.pallas_call(
-        third_kernel,
+        partial(second_kernel, unroll),
         out_shape=(
-            shape((8, *ea.shape[1:]), BF),
-            shape((8, *eo.shape[1:]), BF),
+            shape((S, ca, S), BF),
+            shape((S, co, S), BF),
+            shape((8, ca, S), BF),
+            shape((8, co, S), BF),
         ),
-        in_specs=[hbm] * 2,
-        out_specs=(hbm,) * 2,
-        scratch_shapes=EIGHT + [DMA],
-        compiler_params=pltpu.CompilerParams(collective_id=2, has_side_effects=True),
-        name="third_exchange",
-    )(ea, eo)
+        in_specs=[sm, sm] + [hbm] * 4 + [vm] * 5,
+        out_specs=(vm, vm, hbm, hbm),
+        scratch_shapes=[bf(S, ca, S), bf(S, co, S), bf(8, CS, S), bf(8, CS, S), bf(2 * S, CS, S), bf(S, CS, S)]
+        + [bf(8, ca, S), bf(8, CS, S)]
+        + [bf(8, ca, S), bf(8, CS, S), bf(8, co, S), bf(8, CS, S)]
+        + [bf(4, ca, S), bf(4, CS, S), bf(4, co, S), bf(4, CS, S)]
+        + [VMEM((2, ca, 2 * S), F32), VMEM((2, co, 2 * S), F32)]
+        + [bf(4, ca, S), bf(4, co, S), bf(2, CS, S)]
+        + [bf(4, ca, S), bf(4, ca, S), bf(4, co, S), bf(4, CS, S)]
+        + [DMA((2,)), DMA((2,))]
+        + [DMA((2, 8))] * 4
+        + [DMA((3,))],
+        compiler_params=pltpu.CompilerParams(collective_id=1, has_side_effects=True),
+        name="second_exchange",
+    )(slots, turn, back, es, xa, xo, sea, ha, ho, wa, wo)
 
 
 def taps(weight):
@@ -744,17 +711,14 @@
     wa2 = taps(jnp.take(atmos_w2, order, axis=0))
     wo1, wo2 = taps(ocean_w1), taps(ocean_w2)
     weight = lax.reduce_precision(block_weight[:, 0], 8, 7)
-    xa, xo, ea, eo, pay, meta, common, slots = prepare(
+    pay, meta, common, slots = prepare(
         turn, block_target[:, 0], block_patch[:, 0], weight, atmos_state, ocean_state, mask
     )
-    pay_in, meta_in, ha, ho = first_exchange(pay, meta, ea, eo)
-    patch_in = meta_in[:, 0, :2].reshape(2 * S).astype(jnp.int32)
-    weight_in = meta_in[:, 0, 2:4].reshape(2 * S)
-    sea, es, back = remap(turn, patch_in, weight_in, pay_in, common)
-    hs, force, hf = second_exchange(slots, back, es)
-    hid_a, ea2 = hidden_conv(False, turn, [xa, sea], [ha, hs], wa1, 16)
-    hid_o, eo2 = hidden_conv(True, edge, [xo, force], [ho, hf], wo1, 16)
-    ha2, ho2 = third_exchange(ea2, eo2)
+    pay_in, meta_in, xa, xo, ha, ho = first_exchange(turn, mask, pay, meta, atmos_state, ocean_state)
+    sea, es, back = remap(turn, meta_in, pay_in, common)
+    hid_a, hid_o, ha2, ho2 = second_exchange(
+        slots, turn, back, es.astype(BF), xa, xo, sea, ha, ho, wa1, wo1, 16
+    )
     atmos_out = out_conv(False, turn, hid_a, ha2, wa2, atmos_state, mask, 8)
     ocean_out = out_conv(True, edge, hid_o, ho2, wo2, ocean_state, mask, 8)
     return atmos_out, ocean_out

time: 202 us -> 162 us (0.80)
  Pallas kernels: 188 us -> 150 us
  local copies, waits for them, and re-layouts: 8.33 us -> 5.77 us
    pallas_call x5 -> x2, Pallas kernels: 104 us -> 70.3 us  [the longest x1 65.1 us: second_exchange(): pl.pallas_call(partial(second_kernel, unroll), out_shape=(shape((S, ca, S...]
    pallas_call x1, Pallas kernels: 15.8 us -> 6.85 us  [remap(): pl.pallas_call(remap_kernel, out_shape=(shape((S, CS, S), BF), shape((4,...]
    pallas_call x1, Pallas kernels: 33.3 us -> 38 us  [first_exchange(): pl.pallas_call(first_kernel, out_shape=(shape(pay.shape, BF), shape(meta....]
where the time goes in v1:
time: 162 us; the launch traced here: 161 us
  Pallas kernels  150 us (93%)
  local copies, waits for them, and re-layouts  5.77 us (4%)
  other arithmetic  3.78 us (2%)
    pallas_call x1, Pallas kernels, second_exchange(): pl.pallas_call(partial(second_kernel, unroll), out_shape=(shape((S, ca, S...  65.1 us
    pallas_call x1, Pallas kernels, first_exchange(): pl.pallas_call(first_kernel, out_shape=(shape(pay.shape, BF), shape(meta....  38 us
    pallas_call x2, Pallas kernels, out_conv(): pl.pallas_call(partial(out_kernel, ocean, unroll), out_shape=jax.ShapeDty...  35.3 us
    pallas_call x1, Pallas kernels, remap(): pl.pallas_call(remap_kernel, out_shape=(shape((S, CS, S), BF), shape((4,...  6.85 us
    pallas_call x1, Pallas kernels, prepare(): pl.pallas_call(prep_kernel, grid=(1,), out_shape=(shape((2 * S, CS, S), B...  5.2 us

profile of v1, /device:TPU:0, one launch (start us, length us, event | category | flops | bytes accessed | tf_op | source)
XLA Modules:
  0.0 161.4 jit_solution(7987882039076105349)
XLA Ops:
  0.6 0.0 copy-start
  1.3 0.7 convert_element_type.8
  2.0 0.7 copy.19.mask_ref
  2.8 1.1 reduce-precision_bitcast_fusion.weight_ref
  3.9 5.2 %prepare.1 = (bf16[256,16,128]{2,1,0:T(8,128)(2,1)}, f32[256,1,128]{2,1,0:T(1,128)}, bf16[16,128,128]{2,1,0:T(8,128)(2,1)}, s32[128]{0:T(128)}) custom-call(s32[1]{0:T(128)} %bitcast.36.turn_ref, s32[128]{0:T(128)} %bitcast.55, s32[128]{0:T(128)} %bitcast.56, f32[128]{0:T(128)} %reduce-precision_bitcast_fusion.weight_ref, bf16[128,128,128]{2,1,0:T(8,128)(2,1)} %base_ref.2, ...), custom_call_target="tpu_custom_call" | custom-call | tf_op jit(solution)/shard_map/prepare/pallas_call | solution.py:303
  9.1 0.0 copy-start.4
  9.1 38.0 %first_exchange.1 = (bf16[256,16,128]{2,1,0:T(8,128)(2,1)}, f32[256,1,128]{2,1,0:T(1,128)}, bf16[128,128,128]{2,1,0:T(8,128)(2,1)}, bf16[128,64,128]{2,1,0:T(8,1...) custom-call(s32[1]{0:T(128)} %bitcast.37.turn_ref, bf16[128,128]{1,0:T(8,128)(2,1)} %copy.19.mask_ref, ...), custom_call_target="tpu_custom_call" | custom-call | tf_op jit(solution)/shard_map/first_exchange/pallas_call | solution.py:568
  47.1 0.0 copy-start.2
  47.1 6.8 %remap.1 = (bf16[128,16,128]{2,1,0:T(8,128)(2,1)}, f32[4,16,128]{2,1,0:T(8,128)}, bf16[256,16,128]{2,1,0:T(8,128)(2,1)}) custom-call(s32[1]{0:T(128)} %bitcast.38.turn_ref, f32[256,1,128]{2,1,0:T(1,128)} %get-tuple-element.22.meta_ref, bf16[256,16,128]{2,1,0:T(8,128)(2,1)} %get-tuple-element.23.in_ref, bf16[16,128,128]{2,1,0:T(8,128)(2,1)} %get-tuple-element.24.common_ref), custom_call_target="tpu_custom_call" | custom-call | tf_op jit(solution)/shard_map/remap/pallas_call | solution.py:360
  54.0 1.4 convert_element_type.10.es
  55.3 0.0 copy-done.4
  55.4 0.0 copy-done
  55.4 0.6 gather_fusion
  56.0 0.1 squeeze.14
  56.1 0.1 copy.21
  56.2 0.3 copy_select_fusion
  56.5 0.1 copy.37
  56.6 0.9 copy.24.wa_ref
  57.5 0.0 copy-done.2
  57.5 0.1 copy.40
  57.6 0.8 reshape.75.wo_ref
  58.4 0.0 copy-start.3
  58.4 65.1 %second_exchange.1 = (bf16[128,128,128]{2,1,0:T(8,128)(2,1)}, bf16[128,64,128]{2,1,0:T(8,128)(2,1)}, bf16[8,128,128]{2,1,0:T(8,128)(2,1)}, bf16[8,64,128]{2,1,0:T(8,128)(2,1)}) custom-call(s32[128]{0:T(128)} %get-tuple-element.19.slot_ref, s32[1]{0:T(128)} %bitcast.39.turn_ref, bf16[256,16,128]{2,1,0:T(8,128)(2,1)} %get-tuple-element.25.back, ...), custom_call_target="tpu_custom_call" | custom-call | tf_op jit(solution)/shard_map/second_exchange/pallas_call | solution.py:662
  123.5 0.0 copy-start.1
  123.5 0.0 copy-done.3
  123.5 0.1 copy.39
  123.6 0.8 reshape.79.w_ref
  124.5 12.9 %out_ocean.1 = bf16[64,128,128]{2,1,0:T(8,128)(2,1)} custom-call(s32[1]{0:T(128)} %bitcast.14.mode_ref, bf16[128,64,128]{2,1,0:T(8,128)(2,1)} %get-tuple-element.34.hid_ref, bf16[8,64,128]{2,1,0:T(8,128)(2,1)} %get-tuple-element.35.halo_ref, bf16[192,192]{1,0:T(8,128)(2,1)} %reshape.79.w_ref, bf16[64,128,128]{2,1,0:T(8,128)(2,1)} %base_ref.3, ...), custom_call_target="tpu_custom_call" | custom-call | tf_op jit(solution)/shard_map/out_ocean/pallas_call | solution.py:243
  137.4 0.0 copy-done.1
  137.4 0.6 gather_fusion.1
  138.0 0.3 copy_select_fusion.1
  138.3 0.7 copy.38
  139.0 22.4 %out_atmos.1 = bf16[128,128,128]{2,1,0:T(8,128)(2,1)} custom-call(s32[1]{0:T(128)} %bitcast.40.mode_ref, bf16[128,128,128]{2,1,0:T(8,128)(2,1)} %get-tuple-element.32.hid_ref, bf16[8,128,128]{2,1,0:T(8,128)(2,1)} %get-tuple-element.33.halo_ref, bf16[384,384]{1,0:T(8,128)(2,1)} %bitcast.48, bf16[128,128,128]{2,1,0:T(8,128)(2,1)} %base_ref.2, ...), custom_call_target="tpu_custom_call" | custom-call | tf_op jit(solution)/shard_map/out_atmos/pallas_call | solution.py:243
  (5 shorter events, 0.1 us)
Async XLA Ops:
  0.6 54.7 %copy-start = (bf16[9,128,144]{1,2,0:T(8,128)(2,1)S(1)}, bf16[9,128,144]{1,2,0:T(8,128)(2,1)}, u32[]{:S(2)}) copy-start(bf16[9,128,144]{1,2,0:T(8,128)(2,1)} %param.19) | copy-start | bytes 995332
  9.1 46.2 %copy-start.4 = (s32[4,9]{1,0:T(4,128)S(1)}, s32[4,9]{1,0:T(4,128)}, u32[]{:S(2)}) copy-start(s32[4,9]{1,0:T(4,128)} %constant.45.clone) | copy-start | bytes 436
  47.1 10.4 %copy-start.2 = (bf16[9,64,80]{2,1,0:T(8,128)(2,1)S(1)}, bf16[9,64,80]{2,1,0:T(8,128)(2,1)}, u32[]{:S(2)}) copy-start(bf16[9,64,80]{2,1,0:T(8,128)(2,1)} %param.21) | copy-start | bytes 276484
  58.4 65.1 %copy-start.3 = (bf16[9,64,64]{2,1,0:T(8,128)(2,1)S(1)}, bf16[9,64,64]{2,1,0:T(8,128)(2,1)}, u32[]{:S(2)}) copy-start(bf16[9,64,64]{2,1,0:T(8,128)(2,1)} %param.22) | copy-start | bytes 221188
  123.5 13.9 %copy-start.1 = (bf16[9,128,128]{2,1,0:T(8,128)(2,1)S(1)}, bf16[9,128,128]{2,1,0:T(8,128)(2,1)}, u32[]{:S(2)}) copy-start(bf16[9,128,128]{2,1,0:T(8,128)(2,1)} %param.20) | copy-start | bytes 884740

commit v2 on v1

--- a/solution.py
+++ b/solution.py
@@ -12,6 +12,7 @@
 S = 128
 CS = 16
 MESH = pl.DeviceIdType.MESH
+DMA = pltpu.SemaphoreType.DMA
 VMEM = pltpu.VMEM
 SMEM = pltpu.SMEM
 
@@ -192,31 +193,106 @@
     lax.fori_loop(0, 4, sixteen, 0)
 
 
-def hidden_rows(parts, sides, runs, w_ref, hid_ref, carry, cols, own, unroll):
+def fed_rows(parts, sides, runs, w_ref, outs, carry, feed, held, finish, flush, unroll):
+    first = [lanes(p.shape[1]) == 0 for p in parts]
+    last = [lanes(p.shape[1]) == S - 1 for p in parts]
+    total = sum(p.shape[1] for p in parts)
+    for side, run in zip(sides, runs):
+        run[0] = side[LEFT]
+        run[1] = roll(side[LEFT], 64)
+        run[2] = roll(side[RIGHT], 1)
+        run[3] = roll(side[RIGHT], 65)
+
+    def build(r, first_row, end, slot):
+        at = 0
+        for n, (p, side, run) in enumerate(zip(parts, sides, runs)):
+            la, lb, ra, rb = run[0], run[1], run[2], run[3]
+            run[0], run[1], run[2], run[3] = roll(la, -1), roll(lb, -1), roll(ra, -1), roll(rb, -1)
+            if first_row:
+                xa, la, ra = side[UP], side[UL], side[UR]
+            else:
+                xa = p[jnp.minimum(r - 1, S - 1)] if end is not None else p[r - 1]
+            if end is None:
+                xb = p[r + 63]
+            else:
+                xb = jnp.where(end, side[DOWN], p[jnp.minimum(r + 63, S - 1)])
+                lb, rb = jnp.where(end, side[DL], lb), jnp.where(end, side[DR], rb)
+            size = p.shape[1]
+            for half, (x, l, r_) in enumerate(((xa, la, ra), (xb, lb, rb))):
+                cols = slice(half * S, (half + 1) * S)
+                feed[slot, at : at + size, cols] = roll(jnp.where(last[n], l, x), 1)
+                feed[slot, total + at : total + at + size, cols] = x
+                feed[slot, 2 * total + at : 2 * total + at + size, cols] = roll(jnp.where(first[n], r_, x), -1)
+            at += size
+
+    o = outs
+    build(0, True, None, 0)
+    build(1, False, None, 1)
+    p0 = dot(w_ref[...], feed[0])
+    build(2, False, None, 0)
+    p1 = dot(w_ref[...], feed[1])
+    carry[0] = p0[:o] + p1[o : 2 * o]
+    carry[1] = p1[:o]
+    if held is not None:
+        held[...] = jnp.zeros_like(held)
+
+    def sixteen(g, _):
+        def body(i, _):
+            done, near = carry[0], carry[1]
+            before = None if held is None else held[...]
+            for u in range(unroll):
+                y = g * 16 + i * unroll + u
+                p = dot(w_ref[...], feed[u % 2])
+                build(y + 3, False, y >= 62 if u >= unroll - 2 else None, (u + 1) % 2)
+                if held is not None or u:
+                    finish(y - 1, before)
+                before = done + p[2 * o :]
+                done, near = near + p[o : 2 * o], p[:o]
+            if held is None:
+                finish(y, before)
+            else:
+                held[...] = before
+            carry[0], carry[1] = done, near
+            return 0
+
+        lax.fori_loop(0, 16 // unroll, body, 0)
+        if flush is not None:
+            flush(g)
+        return 0
+
+    lax.fori_loop(0, 4, sixteen, 0)
+    if held is not None:
+        finish(63, held[...])
+
+
+def hidden_rows(parts, sides, runs, w_ref, hid_ref, carry, cols, own, unroll, feed=None, held=None):
     outs = hid_ref.shape[1]
     first, last = lanes(outs) == 0, lanes(outs) == S - 1
+    cols[...] = jnp.zeros_like(cols)
 
     def finish(y, both):
         for half in range(2):
             v = jax.nn.gelu(both[:, half * S : (half + 1) * S], approximate=True).astype(BF)
-            hid_ref[y + 64 * half] = v
+            hid_ref[(y if feed is None else jnp.maximum(y, 0)) + 64 * half] = v
             cols[half] = roll(jnp.where(first, v, cols[half]), -1)
             cols[2 + half] = jnp.where(last, v, roll(cols[2 + half], -1))
 
-    conv_rows(parts, sides, runs, w_ref, outs, carry, finish, None, unroll)
+    if feed is None:
+        conv_rows(parts, sides, runs, w_ref, outs, carry, finish, None, unroll)
+    else:
+        fed_rows(parts, sides, runs, w_ref, outs, carry, feed, held, finish, None, unroll)
     upper = lanes(outs) >= 64
     own[UP], own[DOWN] = hid_ref[0], hid_ref[S - 1]
     own[LEFT] = jnp.where(upper, cols[1], roll(cols[0], 64))
     own[RIGHT] = jnp.where(upper, cols[3], roll(cols[2], 64))
 
 
-def out_kernel(ocean, unroll, mode_ref, hid_ref, halo_ref, w_ref, base_ref, mask_ref, out_ref, side, run, carry, stage):
-    mode = mode_ref[0]
-    if ocean:
-        ocean_sides(mode, halo_ref, side)
-    else:
-        select_sides(TO_STORED, mode, halo_ref, side)
-    outs = hid_ref.shape[1]
+def out_rows(ocean, hid, side, run, w_ref, base, mask_ref, out, target, sem, carry, feed, stage, unroll):
+    outs = hid.shape[1]
+
+    def part(g, half):
+        rows = pl.ds(pl.multiple_of(g * 16 + 64 * half, 16), 16)
+        return pltpu.make_async_copy(out.at[:, rows, :], target.at[:, rows, :], sem.at[g, half])
 
     def finish(y, both):
         place = lax.rem(y, 16)
@@ -226,33 +302,69 @@
     def flush(g):
         for half in range(2):
             rows = pl.ds(pl.multiple_of(g * 16 + 64 * half, 16), 16)
-            base = base_ref[:, rows, :].astype(F32)
+            kept = base[:, rows, :].astype(F32)
             summed = stage[half].reshape(outs, 16, S)
             if ocean:
                 gate = mask_ref[rows, :].astype(F32)[None]
-                out_ref[:, rows, :] = (gate * (gate * base + summed)).astype(BF)
+                out[:, rows, :] = (gate * (gate * kept + summed)).astype(BF)
             else:
-                out_ref[:, rows, :] = (base + summed).astype(BF)
-
-    conv_rows([hid_ref], [side], [run], w_ref, outs, carry, finish, flush, unroll)
-
-
-def out_conv(ocean, mode, hidden, halo, weight, base, mask, unroll):
-    outs = hidden.shape[1]
-    vm = pl.BlockSpec(memory_space=VMEM)
+                out[:, rows, :] = (kept + summed).astype(BF)
+            part(g, half).start()
+
+    fed_rows([hid], [side], [run], w_ref, outs, carry, feed, None, finish, flush, unroll)
+
+    def wait():
+        for g in range(4):
+            for half in range(2):
+                part(g, half).wait()
+
+    return wait
+
+
+def outs_kernel(
+    turn_ref, edge_ref, hid_a, hid_o, ha_ref, ho_ref, wa_ref, wo_ref, base_a, base_o, mask_ref, out_a, out_o,
+    h_a, h_o, b_a, b_o, o_a, o_o, side_a, side_o, run_a, run_o, carry_a, carry_o, feed_a, feed_o, stage_a, stage_o,
+    loads, sem_a, sem_o,
+):
+    pairs = ((hid_o, h_o), (base_o, b_o), (hid_a, h_a), (base_a, b_a))
+    copies = [pltpu.make_async_copy(src, dst, loads.at[n]) for n, (src, dst) in enumerate(pairs)]
+    for each in copies:
+        each.start()
+    ocean_sides(edge_ref[0], ho_ref, side_o)
+    select_sides(TO_STORED, turn_ref[0], ha_ref, side_a)
+    copies[0].wait()
+    copies[1].wait()
+    wait_o = out_rows(True, h_o, side_o, run_o, wo_ref, b_o, mask_ref, o_o, out_o, sem_o, carry_o, feed_o, stage_o, 8)
+    copies[2].wait()
+    copies[3].wait()
+    wait_a = out_rows(False, h_a, side_a, run_a, wa_ref, b_a, mask_ref, o_a, out_a, sem_a, carry_a, feed_a, stage_a, 4)
+    wait_o()
+    wait_a()
+
+
+def final_convs(turn, edge, hid_a, hid_o, ha, ho, wa, wo, base_a, base_o, mask):
+    hbm, vm, sm = (pl.BlockSpec(memory_space=m) for m in (pl.ANY, VMEM, SMEM))
+    ca, co = hid_a.shape[1], hid_o.shape[1]
+    scratch = []
+    for make in (
+        lambda c: VMEM((S, c, S), BF),
+        lambda c: VMEM((c, S, S), BF),
+        lambda c: VMEM((c, S, S), BF),
+        lambda c: VMEM((8, c, S), BF),
+        lambda c: VMEM((4, c, S), BF),
+        lambda c: VMEM((2, c, 2 * S), F32),
+        lambda c: VMEM((2, 3 * c, 2 * S), BF),
+        lambda c: VMEM((2, c * 16, S), F32),
+    ):
+        scratch += [make(ca), make(co)]
     return pl.pallas_call(
-        partial(out_kernel, ocean, unroll),
-        out_shape=jax.ShapeDtypeStruct((outs, S, S), BF),
-        in_specs=[pl.BlockSpec(memory_space=SMEM)] + [vm] * 5,
-        out_specs=vm,
-        scratch_shapes=[
-            VMEM((8, outs, S), BF),
-            VMEM((4, outs, S), BF),
-            VMEM((2, outs, 2 * S), F32),
-            VMEM((2, outs * 16, S), F32),
-        ],
-        name="out_ocean" if ocean else "out_atmos",
-    )(mode, hidden, halo, weight, base, mask)
+        outs_kernel,
+        out_shape=(jax.ShapeDtypeStruct((ca, S, S), BF), jax.ShapeDtypeStruct((co, S, S), BF)),
+        in_specs=[sm, sm, hbm, hbm] + [vm] * 4 + [hbm, hbm, vm],
+        out_specs=(hbm, hbm),
+        scratch_shapes=scratch + [DMA((4,)), DMA((4, 2)), DMA((4, 2))],
+        name="final_convs",
+    )(turn, edge, hid_a, hid_o, ha, ho, wa, wo, base_a, base_o, mask)
 
 
 def prep_kernel(
@@ -316,59 +428,39 @@
     )(turn, target, patch, weight, atmos, ocean, mask)
 
 
-def remap_kernel(
-    turn_ref, meta_ref, in_ref, common_ref, sea_ref, es_ref, back_ref, wide, total, spread
-):
-    turn = turn_ref[0]
+def remap_blocks(turn, meta_ref, in_ref, common_ref, sea_ref, side_ref, back_ref, wide, total, spread, edges):
+    high, odd = turn >= 2, (turn % 2) == 1
     meta = meta_ref[...].reshape(2 * S, S)
     spot = jnp.broadcast_to(meta[:, 0:1], (2 * S, S))
     share = jnp.broadcast_to(meta[:, 1:2], (2 * S, S))
-    faces = spot == lax.broadcasted_iota(jnp.int32, (2 * S, S), 1).astype(F32)
-    pick = jnp.where(faces, 1.0, 0.0).astype(BF)
+    row = lax.broadcasted_iota(jnp.int32, (2 * S, S), 1)
+    pick = jnp.where(spot == row.astype(F32), 1.0, 0.0).astype(BF)
+    faces = spot == jnp.where(high, S - 1 - row, row).astype(F32)
     spread[...] = dot_nt(eye(), jnp.where(faces, share, 0.0).astype(BF)).astype(BF)
     amount = jnp.maximum(dot(spread[...], jnp.ones((2 * S, S), BF)), 1.0)
     wide[...] = in_ref[...].astype(F32).reshape(wide.shape)
     sides = lax.broadcasted_iota(jnp.int32, (16, S), 0)
     along = lax.broadcasted_iota(jnp.int32, (16, S), 1)
     ends = jnp.where(along == jnp.where(sides < 2, sides * (S - 1), -1), 1.0, 0.0).astype(BF)
+    plain, turned = eye().astype(F32), anti().astype(F32)
+    upright = jnp.where(high, turned, plain).astype(BF)
+    after = jnp.where(turn == 2, turned, plain).astype(BF)
+    ahead = jnp.where(turn == 1, turned, plain).astype(BF)
     for c in range(CS):
         strip = pl.ds(c, 2 * S, stride=CS)
         blocks = wide[strip, :].astype(BF)
         v = (dot(spread[...], blocks) / amount).astype(BF)
         wide[strip, :] = dot(pick, common_ref[c])
-        total[pl.ds(c, S, stride=CS), :] = v.astype(F32)
-        edge = dot_nt(ends, v)
-        es_ref[LEFT, pl.ds(c, 1), :] = edge[0:1]
-        es_ref[RIGHT, pl.ds(c, 1), :] = edge[1:2]
+        total[pl.ds(c, S, stride=CS), :] = jnp.where(odd, dot_nt(ahead, v), dot(v, after))
+        edge = dot(dot_nt(ends, v).astype(BF), upright)
+        low_row, high_row = v.astype(F32)[0:1], v.astype(F32)[S - 1 : S]
+        edges[UP, pl.ds(c, 1), :] = jnp.where(high, high_row, low_row)
+        edges[DOWN, pl.ds(c, 1), :] = jnp.where(high, low_row, high_row)
+        edges[LEFT, pl.ds(c, 1), :] = edge[0:1]
+        edges[RIGHT, pl.ds(c, 1), :] = edge[1:2]
+    side_ref[...] = edges[...].astype(BF)
     back_ref[...] = wide[...].reshape(2 * S, CS, S).astype(BF)
-    es_ref[UP] = total[pl.ds(0, CS), :]
-    es_ref[DOWN] = total[pl.ds((S - 1) * CS, CS), :]
-    for quarter in range(1, 4):
-
-        @pl.when(turn == quarter)
-        def _():
-            for c in range(CS):
-                strip = pl.ds(c, S, stride=CS)
-                total[strip, :] = turn_matrix(total[strip, :].astype(BF), quarter)
-
     sea_ref[...] = total[...].reshape(S, CS, S).astype(BF)
-
-
-def remap(turn, meta, incoming, common):
-    sm, vm = pl.BlockSpec(memory_space=SMEM), pl.BlockSpec(memory_space=VMEM)
-    shape = jax.ShapeDtypeStruct
-    return pl.pallas_call(
-        remap_kernel,
-        out_shape=(
-            shape((S, CS, S), BF),
-            shape((4, CS, S), F32),
-            shape((2 * S, CS, S), BF),
-        ),
-        in_specs=[sm] + [vm] * 3,
-        out_specs=(vm,) * 3,
-        scratch_shapes=[VMEM((2 * S * CS, S), F32), VMEM((S * CS, S), F32), VMEM((S, 2 * S), BF)],
-        name="remap",
-    )(turn, meta, incoming, common)
 
 
 class Exchange:
@@ -448,31 +540,40 @@
     return f * n_tile + t, lax.axis_size("face") * n_tile, n_tile
 
 
+def each_peer(act):
+    f, t = lax.axis_index("face"), lax.axis_index("tile")
+    n_face, n_tile = lax.axis_size("face"), lax.axis_size("tile")
+
+    def wrapped(at, count):
+        return jnp.where(at >= count, at - count, at)
+
+    def one(df, dt):
+        act(wrapped(f + df, n_face), wrapped(t + dt, n_tile))
+        return 0
+
+    lax.fori_loop(1, n_tile, lambda dt, _: one(0, dt), 0)
+    lax.fori_loop(1, n_face, lambda df, _: lax.fori_loop(0, n_tile, lambda dt, _: one(df, dt), 0), 0)
+
+
 def meet_all():
     me, count, n_tile = place()
     barrier = pltpu.get_barrier_semaphore()
-
-    def greet(i, _):
-        peer = (me + i) % count
-        pl.semaphore_signal(barrier, inc=1, device_id=(peer // n_tile, peer % n_tile), device_id_type=MESH)
-        return 0
-
-    lax.fori_loop(1, count, greet, 0)
+    each_peer(lambda face, tile: pl.semaphore_signal(barrier, inc=1, device_id=(face, tile), device_id_type=MESH))
     pl.semaphore_wait(barrier, count - 1)
 
 
 def everyone(src, dst, rows, send, recv, near):
     me, count, n_tile = place()
 
-    def copy(peer):
-        return pltpu.make_async_remote_copy(
-            src_ref=src.at[pl.ds(peer * rows, rows)],
+    def send_to(face, tile):
+        pltpu.make_async_remote_copy(
+            src_ref=src.at[pl.ds((face * n_tile + tile) * rows, rows)],
             dst_ref=dst.at[pl.ds(me * rows, rows)],
             send_sem=send,
             recv_sem=recv,
-            device_id=(peer // n_tile, peer % n_tile),
+            device_id=(face, tile),
             device_id_type=MESH,
-        )
+        ).start()
 
     own = pltpu.make_async_copy(src.at[pl.ds(me * rows, rows)], dst.at[pl.ds(me * rows, rows)], near)
     other = (lax.axis_index("face"), (lax.axis_index("tile") + 1) % n_tile)
@@ -486,11 +587,7 @@
     )
 
     def start():
-        def one(i, _):
-            copy((me + i) % count).start()
-            return 0
-
-        lax.fori_loop(1, count, one, 0)
+        each_peer(send_to)
         own.start()
 
     def wait():
@@ -501,26 +598,28 @@
     return start, wait
 
 
-DMA = pltpu.SemaphoreType.DMA
-EIGHT = [DMA((8,))] * 4
-
-
-def first_kernel(
-    turn_ref, mask_ref, pay, meta, atmos, ocean, pay_in, meta_in, xa_ref, xo_ref, ha, ho,
-    held_a, held_o, wide_a, wide_o, cols_a, cols_o, own_a, flip_a, side_a, own_o,
-    loads, wide, flat, sa, ra, so, ro, near,
+def main_kernel(
+    slot_ref, turn_ref, mask_ref, common_ref, wa_ref, wo_ref, pay, meta, atmos, ocean,
+    hid_a_out, hid_o_out, ha2, ho2,
+    held_a, held_o, x_a, x_o, hid_a, hid_o, wide_a, wide_o, pay_in, meta_in, back, got, force, sea,
+    wide_s, total, spread, edges, ha, ho, hs, hf, side_s, flip, flip_s,
+    sides_a, sides_s, sides_o, sides_f, run_a, run_s, run_o, run_f,
+    carry_a, carry_o, cols_a, cols_o, cols_f, own_a, own_o, own_f, out_a, out_o, feed, held,
+    loads, sem_m, sem_p, sem_b, sem_xa, sem_xo, sem_s, sem_f, sem_a, sem_o, near, saves,
 ):
+    turn = turn_ref[0]
+
     def load(g, n):
-        source, held = ((atmos, held_a), (ocean, held_o))[n]
+        source, kept = ((atmos, held_a), (ocean, held_o))[n]
         rows = pl.ds(pl.multiple_of(g * 16, 16), 16)
-        return pltpu.make_async_copy(source.at[:, rows, :], held.at[g], loads.at[n, g])
-
-    for n in range(2):
-        for g in range(8):
+        return pltpu.make_async_copy(source.at[:, rows, :], kept.at[g], loads.at[n, g])
+
+    for g in range(8):
+        for n in range(2):
             load(g, n).start()
     meet_all()
-    start_meta, wait_meta = everyone(meta, meta_in, 2, wide.at[0], wide.at[1], near.at[0])
-    start_pay, wait_pay = everyone(pay, pay_in, 2, flat.at[0], flat.at[1], near.at[1])
+    start_meta, wait_meta = everyone(meta, meta_in, 2, sem_m.at[0], sem_m.at[1], near.at[0])
+    start_pay, wait_pay = everyone(pay, pay_in, 2, sem_p.at[0], sem_p.at[1], near.at[1])
     start_meta()
     start_pay()
 
@@ -538,150 +637,104 @@
         wide_o[...] = (held_o[g].astype(F32) * gate).reshape(wide_o.shape)
         for y in range(16):
             v = wide_a[pl.ds(y, wide_a.shape[0] // 16, stride=16), :].astype(BF)
-            xa_ref[g * 16 + y] = v
+            x_a[g * 16 + y] = v
             columns(cols_a, v)
             v = wide_o[pl.ds(y, wide_o.shape[0] // 16, stride=16), :].astype(BF)
-            xo_ref[g * 16 + y] = v
+            x_o[g * 16 + y] = v
             columns(cols_o, v)
         return 0
 
-    cols_a[...] = jnp.zeros_like(cols_a)
-    cols_o[...] = jnp.zeros_like(cols_o)
-    lax.fori_loop(0, 8, sixteen, 0)
-    own_a[UP], own_a[DOWN], own_a[LEFT], own_a[RIGHT] = xa_ref[0], xa_ref[S - 1], cols_a[0], cols_a[1]
-    own_o[UP], own_o[DOWN], own_o[LEFT], own_o[RIGHT] = xo_ref[0], xo_ref[S - 1], cols_o[0], cols_o[1]
-    blended_sides(TO_COMMON, turn_ref[0], own_a, flip_a, side_a)
-    at = Exchange(side_a, ha, False, sa, ra, near.at[2])
-    oc = Exchange(own_o, ho, True, so, ro, near.at[2])
-    at.start()
-    oc.start()
-    wait_meta()
-    wait_pay()
-    at.wait()
-    oc.wait()
-
-
-def first_exchange(turn, mask, pay, meta, atmos, ocean):
-    hbm, vm, sm = (pl.BlockSpec(memory_space=m) for m in (pl.ANY, VMEM, SMEM))
-    shape = jax.ShapeDtypeStruct
-    ca, co = atmos.shape[0], ocean.shape[0]
-    return pl.pallas_call(
-        first_kernel,
-        out_shape=(
-            shape(pay.shape, BF),
-            shape(meta.shape, F32),
-            shape((S, ca, S), BF),
-            shape((S, co, S), BF),
-            shape((8, ca, S), BF),
-            shape((8, co, S), BF),
-        ),
-        in_specs=[sm, vm] + [hbm] * 4,
-        out_specs=(hbm, hbm, vm, vm, hbm, hbm),
-        scratch_shapes=[
-            VMEM((8, ca, 16, S), BF),
-            VMEM((8, co, 16, S), BF),
-            VMEM((ca * 16, S), F32),
-            VMEM((co * 16, S), F32),
-            VMEM((2, ca, S), BF),
-            VMEM((2, co, S), BF),
-            VMEM((4, ca, S), BF),
-            VMEM((4, ca, S), BF),
-            VMEM((4, ca, S), BF),
-            VMEM((4, co, S), BF),
-            DMA((2, 8)),
-            DMA((2,)),
-            DMA((2,)),
-        ]
-        + EIGHT
-        + [DMA((3,))],
-        compiler_params=pltpu.CompilerParams(collective_id=0, has_side_effects=True),
-        name="first_exchange",
-    )(turn, mask, pay, meta, atmos, ocean)
-
-
-def second_kernel(
-    unroll, slot_ref, turn_ref, back, es, xa, xo, sea_ref, ha_ref, ho_ref, wa_ref, wo_ref,
-    hid_a, hid_o, ha2, ho2,
-    x_a, x_o, hs, hf, got, force, flip, flip_s, sides_a, sides_s, sides_o, sides_f,
-    run_a, run_s, run_o, run_f, carry_a, carry_o, cols_a, cols_o, cols_f, own_a, out_a, own_o, own_f,
-    loads, flat, sem_s, sem_f, sem_a, sem_o, near,
-):
-    turn = turn_ref[0]
-    load_a = pltpu.make_async_copy(xa, x_a, loads.at[0])
-    load_o = pltpu.make_async_copy(xo, x_o, loads.at[1])
-    load_a.start()
-    load_o.start()
-    meet_all()
-    start_back, wait_back = everyone(back, got, 2, flat.at[0], flat.at[1], near.at[0])
-    sea = Exchange(es, hs, False, sem_s.at[0], sem_s.at[1], near.at[1])
-    sea.start()
-    start_back()
-    blended_sides(TO_STORED, turn, ha_ref, flip, sides_a)
-    folded_sides(ho_ref, sides_o)
-    load_a.wait()
-    sea.wait()
-    blended_sides(TO_STORED, turn, hs, flip_s, sides_s)
     cols_a[...] = jnp.zeros_like(cols_a)
     cols_o[...] = jnp.zeros_like(cols_o)
     cols_f[...] = jnp.zeros_like(cols_f)
-    hidden_rows([x_a, sea_ref], [sides_a, sides_s], [run_a, run_s], wa_ref, hid_a, carry_a, cols_a, own_a, unroll)
-    blended_sides(TO_COMMON, turn, own_a, flip, out_a)
-    atmos = Exchange(out_a, ha2, False, sem_a.at[0], sem_a.at[1], near.at[1])
-    atmos.start()
-    load_o.wait()
+    lax.fori_loop(0, 8, sixteen, 0)
+    own_a[UP], own_a[DOWN], own_a[LEFT], own_a[RIGHT] = x_a[0], x_a[S - 1], cols_a[0], cols_a[1]
+    own_o[UP], own_o[DOWN], own_o[LEFT], own_o[RIGHT] = x_o[0], x_o[S - 1], cols_o[0], cols_o[1]
+    blended_sides(TO_COMMON, turn, own_a, flip, out_a.at[0])
+    state = Exchange(out_a.at[0], ha, False, sem_xa.at[0], sem_xa.at[1], near.at[2])
+    masked = Exchange(own_o, ho, True, sem_xo.at[0], sem_xo.at[1], near.at[2])
+    state.start()
+    masked.start()
+    wait_meta()
+    wait_pay()
+    remap_blocks(turn, meta_in, pay_in, common_ref, sea, side_s, back, wide_s, total, spread, edges)
+    start_back, wait_back = everyone(back, got, 2, sem_b.at[0], sem_b.at[1], near.at[0])
+    surface = Exchange(side_s, hs, False, sem_s.at[0], sem_s.at[1], near.at[1])
+    surface.start()
+    start_back()
+    state.wait()
+    masked.wait()
+    blended_sides(TO_STORED, turn, ha, flip, sides_a)
+    folded_sides(ho, sides_o)
+    surface.wait()
+    blended_sides(TO_STORED, turn, hs, flip_s, sides_s)
+    hidden_rows([x_a, sea], [sides_a, sides_s], [run_a, run_s], wa_ref, hid_a, carry_a, cols_a, own_a, 2, feed, held)
+    save_a = pltpu.make_async_copy(hid_a, hid_a_out, saves.at[0])
+    save_a.start()
+    blended_sides(TO_COMMON, turn, own_a, flip, out_a.at[1])
+    around_a = Exchange(out_a.at[1], ha2, False, sem_a.at[0], sem_a.at[1], near.at[1])
+    around_a.start()
     wait_back()
     first, last = lanes(CS) == 0, lanes(CS) == S - 1
 
     def put(i, _):
-        for u in range(4):
-            b = i * 4 + u
+        for u in range(8):
+            b = i * 8 + u
             v = got[slot_ref[b]]
             force[b] = v
             cols_f[0] = roll(jnp.where(first, v, cols_f[0]), -1)
             cols_f[1] = jnp.where(last, v, roll(cols_f[1], -1))
         return 0
 
-    lax.fori_loop(0, S // 4, put, 0)
+    lax.fori_loop(0, S // 8, put, 0)
     own_f[UP], own_f[DOWN], own_f[LEFT], own_f[RIGHT] = force[0], force[S - 1], cols_f[0], cols_f[1]
     forcing = Exchange(own_f, hf, True, sem_f.at[0], sem_f.at[1], near.at[2])
     forcing.start()
     forcing.wait()
     folded_sides(hf, sides_f)
-    hidden_rows([x_o, force], [sides_o, sides_f], [run_o, run_f], wo_ref, hid_o, carry_o, cols_o, own_o, unroll)
-    ocean = Exchange(own_o, ho2, True, sem_o.at[0], sem_o.at[1], near.at[2])
-    ocean.start()
-    atmos.wait()
-    ocean.wait()
-
-
-def second_exchange(slots, turn, back, es, xa, xo, sea, ha, ho, wa, wo, unroll):
+    hidden_rows([x_o, force], [sides_o, sides_f], [run_o, run_f], wo_ref, hid_o, carry_o, cols_o, out_o, 16)
+    around_o = Exchange(out_o, ho2, True, sem_o.at[0], sem_o.at[1], near.at[2])
+    around_o.start()
+    save_o = pltpu.make_async_copy(hid_o, hid_o_out, saves.at[1])
+    save_o.start()
+    around_a.wait()
+    around_o.wait()
+    save_a.wait()
+    save_o.wait()
+
+
+def main(slots, turn, mask, common, wa, wo, pay, meta, atmos, ocean):
     hbm, vm, sm = (pl.BlockSpec(memory_space=m) for m in (pl.ANY, VMEM, SMEM))
     shape = jax.ShapeDtypeStruct
-    ca, co = xa.shape[1], xo.shape[1]
+    ca, co = atmos.shape[0], ocean.shape[0]
     bf = lambda *dims: VMEM(dims, BF)
+    fl = lambda *dims: VMEM(dims, F32)
     return pl.pallas_call(
-        partial(second_kernel, unroll),
+        main_kernel,
         out_shape=(
             shape((S, ca, S), BF),
             shape((S, co, S), BF),
             shape((8, ca, S), BF),
             shape((8, co, S), BF),
         ),
-        in_specs=[sm, sm] + [hbm] * 4 + [vm] * 5,
-        out_specs=(vm, vm, hbm, hbm),
-        scratch_shapes=[bf(S, ca, S), bf(S, co, S), bf(8, CS, S), bf(8, CS, S), bf(2 * S, CS, S), bf(S, CS, S)]
-        + [bf(8, ca, S), bf(8, CS, S)]
+        in_specs=[sm, sm] + [vm] * 4 + [hbm] * 4,
+        out_specs=(hbm,) * 4,
+        scratch_shapes=[bf(8, ca, 16, S), bf(8, co, 16, S), bf(S, ca, S), bf(S, co, S), bf(S, ca, S), bf(S, co, S)]
+        + [fl(ca * 16, S), fl(co * 16, S), bf(2 * S, CS, S), fl(2 * S, 1, S)]
+        + [bf(2 * S, CS, S), bf(2 * S, CS, S), bf(S, CS, S), bf(S, CS, S)]
+        + [fl(2 * S * CS, S), fl(S * CS, S), bf(S, 2 * S), fl(4, CS, S)]
+        + [bf(8, ca, S), bf(8, co, S), bf(8, CS, S), bf(8, CS, S), bf(4, CS, S), bf(8, ca, S), bf(8, CS, S)]
         + [bf(8, ca, S), bf(8, CS, S), bf(8, co, S), bf(8, CS, S)]
         + [bf(4, ca, S), bf(4, CS, S), bf(4, co, S), bf(4, CS, S)]
-        + [VMEM((2, ca, 2 * S), F32), VMEM((2, co, 2 * S), F32)]
-        + [bf(4, ca, S), bf(4, co, S), bf(2, CS, S)]
-        + [bf(4, ca, S), bf(4, ca, S), bf(4, co, S), bf(4, CS, S)]
-        + [DMA((2,)), DMA((2,))]
-        + [DMA((2, 8))] * 4
-        + [DMA((3,))],
-        compiler_params=pltpu.CompilerParams(collective_id=1, has_side_effects=True),
-        name="second_exchange",
-    )(slots, turn, back, es, xa, xo, sea, ha, ho, wa, wo)
+        + [fl(2, ca, 2 * S), fl(2, co, 2 * S), bf(4, ca, S), bf(4, co, S), bf(2, CS, S)]
+        + [bf(4, ca, S), bf(4, co, S), bf(4, CS, S), bf(2, 4, ca, S), bf(4, co, S)]
+        + [bf(2, 3 * (ca + CS), 2 * S), fl(ca, 2 * S)]
+        + [DMA((2, 8)), DMA((2,)), DMA((2,)), DMA((2,))]
+        + [DMA((2, 8))] * 6
+        + [DMA((3,)), DMA((2,))],
+        compiler_params=pltpu.CompilerParams(collective_id=0, has_side_effects=True),
+        name="main",
+    )(slots, turn, mask, common, wa, wo, pay, meta, atmos, ocean)
 
 
 def taps(weight):
@@ -714,13 +767,10 @@
     pay, meta, common, slots = prepare(
         turn, block_target[:, 0], block_patch[:, 0], weight, atmos_state, ocean_state, mask
     )
-    pay_in, meta_in, xa, xo, ha, ho = first_exchange(turn, mask, pay, meta, atmos_state, ocean_state)
-    sea, es, back = remap(turn, meta_in, pay_in, common)
-    hid_a, hid_o, ha2, ho2 = second_exchange(
-        slots, turn, back, es.astype(BF), xa, xo, sea, ha, ho, wa1, wo1, 16
+    hid_a, hid_o, ha, ho = main(slots, turn, mask, common, wa1, wo1, pay, meta, atmos_state, ocean_state)
+    atmos_out, ocean_out = final_convs(
+        turn, edge, hid_a, hid_o, ha, ho, wa2, wo2, atmos_state, ocean_state, mask
     )
-    atmos_out = out_conv(False, turn, hid_a, ha2, wa2, atmos_state, mask, 8)
-    ocean_out = out_conv(True, edge, hid_o, ho2, wo2, ocean_state, mask, 8)
     return atmos_out, ocean_out
 
 

time: 162 us -> 134 us (0.83)
  Pallas kernels: 150 us -> 120 us
  local copies, waits for them, and re-layouts: 5.77 us -> 9.23 us
    pallas_call x5 -> x2, Pallas kernels: 145 us -> 116 us  [the longest x1 86.6 us: main(): pl.pallas_call(main_kernel, out_shape=(shape((S, ca, S), BF), shape((S, c...]
    reshape x5, local copies, waits for them, and re-layouts: 2.77 us -> 4.61 us  [taps(): weight.reshape(3, 3, outs, channels).transpose(0, 2, 1, 3)]
where the time goes in v2:
time: 134 us
  Pallas kernels  120 us (90%)
  local copies, waits for them, and re-layouts  9.23 us (7%)
  other arithmetic  3.18 us (2%)
  between operations  1.57 us (1%)
    pallas_call x1, Pallas kernels, main(): pl.pallas_call(main_kernel, out_shape=(shape((S, ca, S), BF), shape((S, c...  86.6 us
    pallas_call x1, Pallas kernels, final_convs(): pl.pallas_call(outs_kernel, out_shape=(jax.ShapeDtypeStruct((ca, S, S), B...  29.1 us
    reshape x5, local copies, waits for them, and re-layouts, taps(): weight.reshape(3, 3, outs, channels).transpose(0, 2, 1, 3)  4.61 us
    pallas_call x1, Pallas kernels, prepare(): pl.pallas_call(prep_kernel, grid=(1,), out_shape=(shape((2 * S, CS, S), B...  4.14 us

profile of v2, /device:TPU:0, one launch (start us, length us, event | category | flops | bytes accessed | tf_op | source)
XLA Modules:
  0.0 133.8 jit_solution(4386587711187000075)
XLA Ops:
  0.6 0.0 copy-start
  1.4 1.2 reduce-precision_bitcast_fusion.weight_ref
  2.6 0.7 fusion
  3.3 0.7 dynamic-slice_reduce_fusion
  4.0 0.7 convert_element_type.5
  4.7 0.1 squeeze.14
  4.8 0.1 copy.20
  4.9 0.7 copy.19.mask_ref
  5.6 1.0 copy.39
  6.6 0.8 reshape.76.wo_ref
  7.4 1.0 copy.38
  8.5 0.8 reshape.79.wo_ref
  9.3 1.6 %gather_fusion.1 = bf16[9,128,128]{2,1,0:T(8,128)(2,1)S(1)} fusion(bf16[9,128,128]{2,1,0:T(8,128)(2,1)} %param.20, s32[1024]{0:T(1024)S(1)} %pad_clamp_fusion), kind=kCustom, calls=%fused_computation.1 | custom fusion | bytes 589860 | tf_op jit(solution)/shard_map/jit(_take)/gather | solution.py:764
  10.8 0.3 copy_select_fusion.1
  11.1 0.8 copy.37
  11.9 0.0 copy-done
  11.9 0.6 gather_fusion
  12.5 0.3 copy_select_fusion
  12.8 0.1 copy.36
  12.9 1.0 copy.24.wa_ref
  13.8 4.1 %prepare.1 = (bf16[256,16,128]{2,1,0:T(8,128)(2,1)}, f32[256,1,128]{2,1,0:T(1,128)}, bf16[16,128,128]{2,1,0:T(8,128)(2,1)}, s32[128]{0:T(128)}) custom-call(s32[1]{0:T(128)} %bitcast.36.turn_ref, s32[128]{0:T(128)} %bitcast.53, s32[128]{0:T(128)} %bitcast.54, f32[128]{0:T(128)} %reduce-precision_bitcast_fusion.weight_ref, bf16[128,128,128]{2,1,0:T(8,128)(2,1)} %base_a.1, ...), custom_call_target="tpu_custom_call" | custom-call | tf_op jit(solution)/shard_map/prepare/pallas_call | solution.py:415
  18.0 86.6 %main.1 = (bf16[128,128,128]{2,1,0:T(8,128)(2,1)}, bf16[128,64,128]{2,1,0:T(8,128)(2,1)}, bf16[8,128,128]{2,1,0:T(8,128)(2,1)}, bf16[8,64,128]{2,1,0:T(8,128)(2,1)}) custom-call(s32[128]{0:T(128)} %get-tuple-element.10.slot_ref, s32[1]{0:T(128)} %bitcast.37.turn_ref, bf16[128,128]{1,0:T(8,128)(2,1)} %copy.19.mask_ref, ...), custom_call_target="tpu_custom_call" | custom-call | tf_op jit(solution)/shard_map/main/pallas_call | solution.py:712
  104.6 29.1 %final_convs.1 = (bf16[128,128,128]{2,1,0:T(8,128)(2,1)}, bf16[64,128,128]{2,1,0:T(8,128)(2,1)}) custom-call(s32[1]{0:T(128)} %bitcast.38.turn_ref, s32[1]{0:T(128)} %bitcast.1.edge_ref, bf16[128,128,128]{2,1,0:T(8,128)(2,1)} %get-tuple-element.14.hid_a, bf16[128,64,128]{2,1,0:T(8,128)(2,1)} %get-tuple-element.15.hid_o, ...), custom_call_target="tpu_custom_call" | custom-call | tf_op jit(solution)/shard_map/final_convs/pallas_call | solution.py:360
  (3 shorter events, 0.0 us)
Async XLA Ops:
  0.6 11.3 %copy-start = (bf16[9,128,144]{1,2,0:T(8,128)(2,1)S(1)}, bf16[9,128,144]{1,2,0:T(8,128)(2,1)}, u32[]{:S(2)}) copy-start(bf16[9,128,144]{1,2,0:T(8,128)(2,1)} %param.19) | copy-start | bytes 995332
